TPU v7x, 32 devices: a whole 2x2x4 slice. The times are simulated.
32 devices in a mesh: gx: 4 (over y, x), gy: 8 (over z, core).
Axes of the slice: x: 2, y: 2, z: 4, core: 2. Of those that a mesh axis runs over, the one named last changes fastest.
Arguments:
- atom_cell: int32 [4, 8, 4096], P('gx', 'gy'), may hold values from 0 to 49151
- atom_frac: float32 [3, 4, 8, 4096], P(None, 'gx', 'gy'), may hold values from 0 to 1
- atom_charge: float32 [4, 8, 4096], P('gx', 'gy'), may hold values from -6 to 6
- atom_count: int32 [4, 8], P('gx', 'gy'), may hold values from 1024 to 4096, as said below
- fine_kernel: float32 [9, 9, 9], replicated, may hold values from -1.8 to 1.8
- middle_kernel: float32 [9, 9, 9], replicated, may hold values from -0.9 to 0.9
- coarse_kernel: float32 [9, 9, 9], replicated, may hold values from -0.36 to 0.36
Outputs:
- potential: float32 [64, 192, 128], P('gx', 'gy')
- forces: float32 [3, 4, 8, 4096], P(None, 'gx', 'gy')
Inputs may be any that keep to these rules, and one draw needn't show every extreme that they name: `atom_count`: slots at or past a block's count hold no atom. At least one block is full in every draw; about a quarter of the blocks are nearly full and the rest hold a quarter to a half of 4096.
All inputs are finite; a program needn't handle non-finite values.
Results may differ from a plain program's by a relative error of at most 0.0003.
Values sent between devices are 32-bit elements; how exact they have to be, the bound alone decides.
A program may use at most 128 MiB of HBM per device.

v0:
```python
import jax
import jax.numpy as jnp
from jax import lax
from jax.sharding import PartitionSpec as P

CX = 16
CY = 24
NZ = 128
ATOMS_DEV = 4096
KERNEL = 9


def from_behind(value, axis, steps):
    count = lax.axis_size(axis)
    pairs = [(source, (source + steps) % count) for source in range(count)]
    return lax.ppermute(value, axis, pairs)


def with_halo(block, sides, width):
    for axis, dim in sides:
        count = lax.axis_size(axis)
        forward = [(i, i + 1) for i in range(count - 1)]
        forward.append((count - 1, 0))
        backward = [(target, source) for source, target in forward]
        low = lax.ppermute(
            lax.slice_in_dim(block, block.shape[dim] - width, None, axis=dim), axis, forward
        )
        high = lax.ppermute(lax.slice_in_dim(block, 0, width, axis=dim), axis, backward)
        block = jnp.concatenate([low, block, high], axis=dim)
    return block


def band_tables(kernel, z_size):
    half_width = KERNEL // 2
    tap_index = lax.broadcasted_iota(jnp.int32, (KERNEL, z_size, z_size), 0)
    z_from = lax.broadcasted_iota(jnp.int32, (KERNEL, z_size, z_size), 1)
    z_to = lax.broadcasted_iota(jnp.int32, (KERNEL, z_size, z_size), 2)
    one_hot = (jnp.mod(z_to + tap_index - half_width, z_size) == z_from).astype(jnp.float32)
    tables = jnp.einsum("abc,cij->abij", kernel, one_hot, precision=lax.Precision.HIGHEST)
    return tables.reshape(KERNEL, KERNEL * z_size, z_size)


def convolve(padded, kernel):
    half_width = KERNEL // 2
    block_rows = padded.shape[0] - 2 * half_width
    block_cols = padded.shape[1] - 2 * half_width
    z_size = padded.shape[2]
    tables = band_tables(kernel, z_size)
    running = jnp.zeros((block_rows * block_cols, z_size), jnp.float32)
    for shift_x in range(KERNEL):
        x_slab = padded[shift_x : shift_x + block_rows]
        joined = jnp.concatenate(
            [x_slab[:, shift_y : shift_y + block_cols, :] for shift_y in range(KERNEL)], axis=2
        )
        running = running + jnp.dot(
            joined.reshape(block_rows * block_cols, KERNEL * z_size),
            tables[shift_x],
            preferred_element_type=jnp.float32,
            precision=lax.Precision.HIGHEST,
        )
    return running.reshape(block_rows, block_cols, z_size)


def halve_axis(segment, dimension):
    length = segment.shape[dimension] - 1
    leading = lax.slice_in_dim(segment, 0, length, 2, dimension)
    middle = lax.slice_in_dim(segment, 1, length + 1, 2, dimension)
    trailing = lax.slice_in_dim(segment, 2, length + 1, 2, dimension)
    return 0.5 * leading + middle + 0.5 * trailing


def restrict(padded):
    half_width = KERNEL // 2
    block_rows = padded.shape[0] - 2 * half_width
    block_cols = padded.shape[1] - 2 * half_width
    segment = padded[
        half_width - 1 : half_width + block_rows, half_width - 1 : half_width + block_cols, :
    ]
    segment = halve_axis(halve_axis(segment, 0), 1)
    segment = jnp.concatenate([segment[:, :, -1:], segment], axis=2)
    return halve_axis(segment, 2)


def refine(extended, dimension):
    length = extended.shape[dimension] - 1
    lower_part = lax.slice_in_dim(extended, 0, length, 1, dimension)
    upper_part = lax.slice_in_dim(extended, 1, length + 1, 1, dimension)
    paired = jnp.stack([lower_part, 0.5 * (lower_part + upper_part)], axis=dimension + 1)
    new_shape = list(lower_part.shape)
    new_shape[dimension] = 2 * length
    return paired.reshape(new_shape)


def prolong(extended):
    extended = jnp.concatenate([extended, extended[:, :, :1]], axis=2)
    return refine(refine(refine(extended, 0), 1), 2)


def upper_rim(grid_in):
    wider = jnp.concatenate([grid_in, from_behind(grid_in[:1], "gx", -1)], axis=0)
    return jnp.concatenate([wider, from_behind(wider[:, :1], "gy", -1)], axis=1)


def corner_terms(atom_cell, atom_frac):
    atom_flat = atom_cell.reshape(-1)
    fractions = atom_frac.reshape(3, -1)
    base_x = atom_flat // (CY * NZ)
    base_y = atom_flat // NZ % CY
    base_z = atom_flat % NZ
    corner_ids = []
    weights = []
    slopes = []
    for corner in range(8):
        raised = [corner >> 2 & 1, corner >> 1 & 1, corner & 1]
        factors = [
            fractions[dimension] if raised[dimension] else 1.0 - fractions[dimension]
            for dimension in range(3)
        ]
        sign_list = [1.0 if raised[dimension] else -1.0 for dimension in range(3)]
        flat_index = ((base_x + raised[0]) * (CY + 1) + base_y + raised[1]) * NZ + (
            base_z + raised[2]
        ) % NZ
        corner_ids.append(flat_index)
        weights.append(factors[0] * factors[1] * factors[2])
        slopes.append(
            jnp.stack(
                [
                    sign_list[0] * factors[1] * factors[2],
                    factors[0] * sign_list[1] * factors[2],
                    factors[0] * factors[1] * sign_list[2],
                ]
            )
        )
    return (corner_ids, jnp.stack(weights), slopes)


def per_device(
    atom_cell, atom_frac, atom_charge, atom_count, fine_kernel, middle_kernel, coarse_kernel
):
    corner_ids, weights, slopes = corner_terms(atom_cell, atom_frac)
    slot_index = lax.broadcasted_iota(jnp.int32, (ATOMS_DEV,), 0)
    is_live = slot_index < atom_count.reshape(())
    live_charge = jnp.where(is_live, atom_charge.reshape(-1), 0.0)
    spread_values = weights * live_charge[None]
    spread = jax.ops.segment_sum(
        spread_values.reshape(-1),
        jnp.stack(corner_ids).reshape(-1),
        num_segments=(CX + 1) * (CY + 1) * NZ,
    ).reshape(CX + 1, CY + 1, NZ)
    from_lower_x = from_behind(spread[CX:], "gx", 1)
    folded = jnp.concatenate([spread[:1] + from_lower_x, spread[1:CX]], axis=0)
    from_lower_y = from_behind(folded[:, CY:], "gy", 1)
    fine_charge = jnp.concatenate([folded[:, :1] + from_lower_y, folded[:, 1:CY]], axis=1)
    fine_padded = with_halo(fine_charge, (("gx", 0), ("gy", 1)), 4)
    middle_charge = restrict(fine_padded)
    middle_padded = with_halo(middle_charge, (("gx", 0), ("gy", 1)), 4)
    coarse_charge = restrict(middle_padded)
    coarse_padded = with_halo(coarse_charge, (("gx", 0), ("gy", 1)), 4)
    coarse_potential = convolve(coarse_padded, coarse_kernel)
    wider = jnp.concatenate([coarse_potential, from_behind(coarse_potential[:1], "gx", -1)], axis=0)
    coarse_extended = jnp.concatenate([wider, from_behind(wider[:, :1], "gy", -1)], axis=1)
    middle_potential = convolve(middle_padded, middle_kernel) + prolong(coarse_extended)
    potential = convolve(fine_padded, fine_kernel) + prolong(upper_rim(middle_potential))
    flat_potential = upper_rim(potential).reshape(-1)
    running = jnp.zeros((3, ATOMS_DEV), jnp.float32)
    for corner in range(8):
        running = running + slopes[corner] * flat_potential[corner_ids[corner]][None]
    forces = (-live_charge[None] * running).reshape(3, 1, 1, ATOMS_DEV)
    return (potential, forces)


def solution(mesh):
    return jax.shard_map(
        per_device,
        mesh=mesh,
        in_specs=(
            P("gx", "gy", None),
            P(None, "gx", "gy", None),
            P("gx", "gy", None),
            P("gx", "gy"),
            P(),
            P(),
            P(),
        ),
        out_specs=(P("gx", "gy", None), P(None, "gx", "gy", None)),
        check_vma=False,
    )
```

profile of v0, /device:TPU:0, one launch (start us, length us, event | category | flops | bytes accessed | tf_op | source)
XLA Modules:
  0.0 543.6 jit_solution(10099245868151225240)
XLA Ops:
  4.4 1.3 fusion.110
  6.0 171.0 %scatter_custom_fusion = f32[54400]{0:T(1024)S(1)} fusion(s32[32768]{0:T(1024)S(1)} %bitcast.327, f32[32768]{0:T(1024)S(1)} %bitcast.328, f32[]{:T(128)} %constant.127.clone.1), kind=kCustom, calls=%fused_computation.194 | custom fusion | flops 32768 | bytes 217604 | tf_op jit(solution)/shard_map/scatter-add | solution.py:145
  177.1 3.0 collective-permute-start
  183.2 3.8 convolution_bitcast_fusion
  187.1 2.9 fusion.115
  190.0 2.0 convolution_bitcast_fusion.1
  192.0 2.2 fusion.116
  195.3 1.5 fusion.117
  204.1 3.9 collective-permute-done.1
  233.3 1.4 collective-permute-done.5
  234.7 3.4 collective-permute-done.4
  238.2 1.5 slice_dynamic-update-slice_fusion.8
  243.8 1.3 slice_dynamic-update-slice_fusion.7
  245.1 1.5 slice_dynamic-update-slice_fusion.6
  246.6 1.4 slice_dynamic-update-slice_fusion.5
  249.8 1.9 collective-permute-start.7
  254.4 1.3 slice_dynamic-update-slice_fusion.3
  259.5 1.6 fusion.128
  261.2 1.6 convolution_add_fusion.7
  262.8 1.6 convolution_add_fusion.6
  264.5 1.6 convolution_add_fusion.5
  266.1 1.6 convolution_add_fusion.4
  267.8 1.6 convolution_add_fusion.3
  269.4 1.6 convolution_add_fusion.2
  272.7 4.0 collective-permute-done.8
  281.4 2.4 collective-permute-start.11
  298.8 1.8 fusion.129
  301.4 1.6 convolution_add_fusion.14
  303.0 1.6 convolution_add_fusion.13
  304.6 1.6 convolution_add_fusion.12
  307.6 1.3 convolution_add_fusion.9
  310.8 3.6 collective-permute-done.12
  330.7 2.4 collective-permute-start.14
  333.1 2.1 collective-permute-done.14
  337.2 2.6 collective-permute-start.16
  339.9 3.1 convolution_add_fusion.1
  343.0 3.3 collective-permute-start.17
  346.2 3.1 convolution_add_fusion
  352.5 3.3 collective-permute-done.18
  356.0 1.4 collective-permute-done.19
  357.5 23.0 %gather_fusion.7 = f32[4096]{0:T(1024)S(1)} fusion(f32[54400]{0:T(1024)S(1)} %reshape.1955, s32[4096]{0:T(1024)S(1)} %copy-done.107), kind=kCustom, calls=%fused_computation.7 | custom fusion | bytes 49152 | tf_op jit(solution)/shard_map/gather | solution.py:167
  380.5 23.0 %gather_fusion.6 = f32[4096]{0:T(1024)S(1)} fusion(f32[54400]{0:T(1024)S(1)} %reshape.1955, s32[4096]{0:T(1024)S(1)} %copy-done.108), kind=kCustom, calls=%fused_computation.6 | custom fusion | bytes 49152 | tf_op jit(solution)/shard_map/gather | solution.py:167
  403.6 23.0 %gather_fusion.5 = f32[4096]{0:T(1024)S(1)} fusion(f32[54400]{0:T(1024)S(1)} %reshape.1955, s32[4096]{0:T(1024)S(1)} %copy-done.109), kind=kCustom, calls=%fused_computation.5 | custom fusion | bytes 49152 | tf_op jit(solution)/shard_map/gather | solution.py:167
  426.7 23.0 %gather_fusion.4 = f32[4096]{0:T(1024)S(1)} fusion(f32[54400]{0:T(1024)S(1)} %reshape.1955, s32[4096]{0:T(1024)S(1)} %copy-done.110), kind=kCustom, calls=%fused_computation.4 | custom fusion | bytes 49152 | tf_op jit(solution)/shard_map/gather | solution.py:167
  449.7 23.0 %gather_fusion.3 = f32[4096]{0:T(1024)S(1)} fusion(f32[54400]{0:T(1024)S(1)} %reshape.1955, s32[4096]{0:T(1024)S(1)} %copy-done.111), kind=kCustom, calls=%fused_computation.3 | custom fusion | bytes 49152 | tf_op jit(solution)/shard_map/gather | solution.py:167
  472.8 23.0 %gather_fusion.2 = f32[4096]{0:T(1024)S(1)} fusion(f32[54400]{0:T(1024)S(1)} %reshape.1955, s32[4096]{0:T(1024)S(1)} %copy-done.112), kind=kCustom, calls=%fused_computation.2 | custom fusion | bytes 49152 | tf_op jit(solution)/shard_map/gather | solution.py:167
  495.8 23.0 %gather_fusion.1 = f32[4096]{0:T(1024)S(1)} fusion(f32[54400]{0:T(1024)S(1)} %reshape.1955, s32[4096]{0:T(1024)S(1)} %broadcast_clamp_fusion.6), kind=kCustom, calls=%fused_computation.1 | custom fusion | bytes 49152 | tf_op jit(solution)/shard_map/gather | solution.py:167
  519.1 23.0 %gather_fusion = f32[4096]{0:T(1024)S(1)} fusion(f32[54400]{0:T(1024)S(1)} %reshape.1955, s32[4096]{0:T(1024)S(1)} %broadcast_clamp_fusion.7), kind=kCustom, calls=%fused_computation | custom fusion | bytes 49152 | tf_op jit(solution)/shard_map/gather | solution.py:167
  (450 shorter events, 100.0 us)
Async XLA Ops:
  0.6 182.6 %copy-start = (f32[9,9,9]{2,1,0:T(8,128)S(1)}, f32[9,9,9]{2,1,0:T(8,128)}, u32[]{:S(2)}) copy-start(f32[9,9,9]{2,1,0:T(8,128)} %param.11) | copy-start | bytes 8752
  0.6 179.5 %copy-start.31 = (f32[3,1,1,4096]{3,2,1,0:T(1,128)S(1)}, f32[3,1,1,4096]{3,2,1,0:T(1,128)}, u32[]{:S(2)}) copy-start(f32[3,1,1,4096]{3,2,1,0:T(1,128)} %param.8) | copy-start | bytes 147460
  0.7 181.6 %copy-start.90 = (s32[1,1,4096]{2,1,0:T(1,128)S(1)}, s32[1,1,4096]{2,1,0:T(1,128)}, u32[]{:S(2)}) copy-start(s32[1,1,4096]{2,1,0:T(1,128)} %param.7) | copy-start | bytes 49156
  177.1 24.2 %collective-permute-start = (f32[1,25,128]{2,1,0:T(8,128)S(1)}, f32[1,25,128]{2,1,0:T(8,128)S(1)}, u32[]{:S(2)}, u32[]{:S(2)}) collective-permute-start(f32[1,25,128]{2,1,0:T(8,128)S(1)} %slice_bitcast_fusion.5), channel_id=1, source_target_pairs={{0,8},{8,16},{16,24},{24,0},{1,9},{9,17},{17,25},{25,1},{2,10},{10... | collective-permute-start | bytes 38408 | tf_op jit(solution)/shard_map/ppermute | solution.py:16
  202.9 5.0 collective-permute-start.1
  208.8 23.8 %collective-permute-start.3 = (f32[4,24,128]{2,1,0:T(8,128)S(1)}, f32[4,24,128]{2,1,0:T(8,128)S(1)}, u32[]{:S(2)}, u32[]{:S(2)}) collective-permute-start(f32[4,24,128]{2,1,0:T(8,128)S(1)} %get-tuple-element.152), channel_id=1, source_target_pairs={{8,0},{16,8},{24,16},{0,24},{9,1},{17,9},{25,17},{1,25},{10,2},{18... | collective-permute-start | bytes 147464 | tf_op jit(solution)/shard_map/ppermute | solution.py:28
  209.9 22.8 %collective-permute-start.2 = (f32[4,24,128]{2,1,0:T(8,128)S(1)}, f32[4,24,128]{2,1,0:T(8,128)S(1)}, u32[]{:S(2)}, u32[]{:S(2)}) collective-permute-start(f32[4,24,128]{2,1,0:T(8,128)S(1)} %get-tuple-element.151), channel_id=1, source_target_pairs={{0,8},{8,16},{16,24},{24,0},{1,9},{9,17},{17,25},{25,1},{2,10},{10... | collective-permute-start | bytes 147464 | tf_op jit(solution)/shard_map/ppermute | solution.py:25
  232.7 2.0 collective-permute-start.5
  232.7 5.4 collective-permute-start.4
  249.8 21.2 %collective-permute-start.7 = (f32[4,12,64]{2,1,0:T(8,128)S(1)}, f32[4,12,64]{2,1,0:T(8,128)S(1)}, u32[]{:S(2)}, u32[]{:S(2)}) collective-permute-start(f32[4,12,64]{2,1,0:T(8,128)S(1)} %get-tuple-element.320), channel_id=1, source_target_pairs={{8,0},{16,8},{24,16},{0,24},{9,1},{17,9},{25,17},{1,25},{10,2},{18... | collective-permute-start | bytes 36872 | tf_op jit(solution)/shard_map/ppermute | solution.py:28
  251.7 19.3 %collective-permute-start.6 = (f32[4,12,64]{2,1,0:T(8,128)S(1)}, f32[4,12,64]{2,1,0:T(8,128)S(1)}, u32[]{:S(2)}, u32[]{:S(2)}) collective-permute-start(f32[4,12,64]{2,1,0:T(8,128)S(1)} %get-tuple-element.319), channel_id=1, source_target_pairs={{0,8},{8,16},{16,24},{24,0},{1,9},{9,17},{17,25},{25,1},{2,10},{10... | collective-permute-start | bytes 36872 | tf_op jit(solution)/shard_map/ppermute | solution.py:25
  271.0 1.7 collective-permute-start.9
  271.1 5.6 %collective-permute-start.8 = (f32[16,4,64]{2,1,0:T(4,128)S(1)}, f32[16,4,64]{2,1,0:T(4,128)S(1)}, u32[]{:S(2)}, u32[]{:S(2)}) collective-permute-start(f32[16,4,64]{2,1,0:T(4,128)S(1)} %get-tuple-element.230), channel_id=1, source_target_pairs={{0,1},{1,2},{2,3},{3,4},{4,5},{5,6},{6,7},{7,0},{8,9},{9,10},{10,1... | collective-permute-start | bytes 49160 | tf_op jit(solution)/shard_map/ppermute | solution.py:25
  281.4 27.7 %collective-permute-start.11 = (f32[4,6,32]{2,1,0:T(8,128)S(1)}, f32[4,6,32]{2,1,0:T(8,128)S(1)}, u32[]{:S(2)}, u32[]{:S(2)}) collective-permute-start(f32[4,6,32]{2,1,0:T(8,128)S(1)} %multiply_add_fusion.6), channel_id=1, source_target_pairs={{8,0},{16,8},{24,16},{0,24},{9,1},{17,9},{25,17},{1,25},{10,2},{18... | collective-permute-start | bytes 9224 | tf_op jit(solution)/shard_map/ppermute | solution.py:28
  283.8 25.4 %collective-permute-start.10 = (f32[4,6,32]{2,1,0:T(8,128)S(1)}, f32[4,6,32]{2,1,0:T(8,128)S(1)}, u32[]{:S(2)}, u32[]{:S(2)}) collective-permute-start(f32[4,6,32]{2,1,0:T(8,128)S(1)} %multiply_add_fusion.6), channel_id=1, source_target_pairs={{0,8},{8,16},{16,24},{24,0},{1,9},{9,17},{17,25},{25,1},{2,10},{10... | collective-permute-start | bytes 9224 | tf_op jit(solution)/shard_map/ppermute | solution.py:25
  309.2 1.6 collective-permute-start.13
  309.3 5.1 collective-permute-start.12
  330.7 4.5 collective-permute-start.14
  335.2 1.3 collective-permute-start.15
  337.2 5.7 %collective-permute-start.16 = (f32[1,12,64]{2,1,0:T(8,128)S(1)}, f32[1,12,64]{2,1,0:T(8,128)S(1)}, u32[]{:S(2)}, u32[]{:S(2)}) collective-permute-start(f32[1,12,64]{2,1,0:T(8,128)S(1)} %slice.2247), channel_id=1, source_target_pairs={{0,24},{8,0},{16,8},{24,16},{1,25},{9,1},{17,9},{25,17},{2,26},{10... | collective-permute-start | bytes 9224 | tf_op jit(solution)/shard_map/ppermute | solution.py:16
  343.0 6.9 %collective-permute-start.17 = (f32[9,1,64]{2,1,0:T(1,128)S(1)}, f32[9,1,64]{2,1,0:T(1,128)S(1)}, u32[]{:S(2)}, u32[]{:S(2)}) collective-permute-start(f32[9,1,64]{2,1,0:T(1,128)S(1)} %pad_maximum_fusion.32), channel_id=1, source_target_pairs={{0,7},{1,0},{2,1},{3,2},{4,3},{5,4},{6,5},{7,6},{8,15},{9,8},{10,9... | collective-permute-start | bytes 6920 | tf_op jit(solution)/shard_map/ppermute | solution.py:16
  351.5 4.3 collective-permute-start.18
  352.5 28.0 %copy-start.30 = (f32[16,24,128]{2,1,0:T(8,128)}, f32[16,24,128]{2,1,0:T(8,128)S(1)}, u32[]{:S(2)}) copy-start(f32[16,24,128]{2,1,0:T(8,128)S(1)} %copy.134) | copy-start | bytes 589828
  355.9 1.5 collective-permute-start.19
  518.8 23.3 %copy-start.79 = (f32[1,1,1,4096]{3,2,1,0:T(1,128)S(1)}, f32[1,1,1,4096]{3,2,1,0:T(1,128)}, u32[]{:S(2)}) copy-start(f32[1,1,1,4096]{3,2,1,0:T(1,128)} %get-tuple-element.331) | copy-start | bytes 49156
  518.9 23.3 %copy-start.80 = (f32[1,1,1,4096]{3,2,1,0:T(1,128)S(1)}, f32[1,1,1,4096]{3,2,1,0:T(1,128)}, u32[]{:S(2)}) copy-start(f32[1,1,1,4096]{3,2,1,0:T(1,128)} %get-tuple-element.332) | copy-start | bytes 49156
  518.9 23.3 %copy-start.81 = (f32[1,1,1,4096]{3,2,1,0:T(1,128)S(1)}, f32[1,1,1,4096]{3,2,1,0:T(1,128)}, u32[]{:S(2)}) copy-start(f32[1,1,1,4096]{3,2,1,0:T(1,128)} %get-tuple-element.333) | copy-start | bytes 49156
  518.9 23.3 %copy-start.82 = (f32[1,1,1,4096]{3,2,1,0:T(1,128)S(1)}, f32[1,1,1,4096]{3,2,1,0:T(1,128)}, u32[]{:S(2)}) copy-start(f32[1,1,1,4096]{3,2,1,0:T(1,128)} %get-tuple-element.334) | copy-start | bytes 49156
  518.9 23.3 %copy-start.83 = (f32[1,1,1,4096]{3,2,1,0:T(1,128)S(1)}, f32[1,1,1,4096]{3,2,1,0:T(1,128)}, u32[]{:S(2)}) copy-start(f32[1,1,1,4096]{3,2,1,0:T(1,128)} %get-tuple-element.335) | copy-start | bytes 49156
  518.9 23.3 %copy-start.84 = (f32[1,1,1,4096]{3,2,1,0:T(1,128)S(1)}, f32[1,1,1,4096]{3,2,1,0:T(1,128)}, u32[]{:S(2)}) copy-start(f32[1,1,1,4096]{3,2,1,0:T(1,128)} %get-tuple-element.336) | copy-start | bytes 49156
  518.9 23.3 %copy-start.85 = (f32[1,1,1,4096]{3,2,1,0:T(1,128)S(1)}, f32[1,1,1,4096]{3,2,1,0:T(1,128)}, u32[]{:S(2)}) copy-start(f32[1,1,1,4096]{3,2,1,0:T(1,128)} %get-tuple-element.337) | copy-start | bytes 49156
  518.9 23.3 %copy-start.86 = (f32[1,1,1,4096]{3,2,1,0:T(1,128)S(1)}, f32[1,1,1,4096]{3,2,1,0:T(1,128)}, u32[]{:S(2)}) copy-start(f32[1,1,1,4096]{3,2,1,0:T(1,128)} %get-tuple-element.338) | copy-start | bytes 49156
  518.9 23.3 %copy-start.87 = (f32[1,1,1,4096]{3,2,1,0:T(1,128)S(1)}, f32[1,1,1,4096]{3,2,1,0:T(1,128)}, u32[]{:S(2)}) copy-start(f32[1,1,1,4096]{3,2,1,0:T(1,128)} %get-tuple-element.339) | copy-start | bytes 49156
  518.9 23.3 %copy-start.88 = (f32[1,1,1,4096]{3,2,1,0:T(1,128)S(1)}, f32[1,1,1,4096]{3,2,1,0:T(1,128)}, u32[]{:S(2)}) copy-start(f32[1,1,1,4096]{3,2,1,0:T(1,128)} %get-tuple-element.340) | copy-start | bytes 49156
  518.9 23.3 %copy-start.89 = (f32[1,1,1,4096]{3,2,1,0:T(1,128)S(1)}, f32[1,1,1,4096]{3,2,1,0:T(1,128)}, u32[]{:S(2)}) copy-start(f32[1,1,1,4096]{3,2,1,0:T(1,128)} %get-tuple-element.341) | copy-start | bytes 49156
  519.0 23.3 %copy-start.91 = (f32[4096]{0:T(1024)S(1)}, f32[4096]{0:T(1024)}, u32[]{:S(2)}) copy-start(f32[4096]{0:T(1024)} %get-tuple-element.8) | copy-start | bytes 49156
  519.0 23.3 %copy-start.94 = (f32[1,1,1,4096]{3,2,1,0:T(1,128)S(1)}, f32[1,1,1,4096]{3,2,1,0:T(1,128)}, u32[]{:S(2)}) copy-start(f32[1,1,1,4096]{3,2,1,0:T(1,128)} %get-tuple-element.20) | copy-start | bytes 49156
  519.0 23.3 %copy-start.95 = (f32[1,1,1,4096]{3,2,1,0:T(1,128)S(1)}, f32[1,1,1,4096]{3,2,1,0:T(1,128)}, u32[]{:S(2)}) copy-start(f32[1,1,1,4096]{3,2,1,0:T(1,128)} %get-tuple-element.21) | copy-start | bytes 49156
  519.0 23.3 %copy-start.96 = (f32[1,1,1,4096]{3,2,1,0:T(1,128)S(1)}, f32[1,1,1,4096]{3,2,1,0:T(1,128)}, u32[]{:S(2)}) copy-start(f32[1,1,1,4096]{3,2,1,0:T(1,128)} %get-tuple-element.342) | copy-start | bytes 49156
  519.0 23.3 %copy-start.97 = (f32[1,1,1,4096]{3,2,1,0:T(1,128)S(1)}, f32[1,1,1,4096]{3,2,1,0:T(1,128)}, u32[]{:S(2)}) copy-start(f32[1,1,1,4096]{3,2,1,0:T(1,128)} %get-tuple-element.321) | copy-start | bytes 49156
  519.0 23.3 %copy-start.98 = (f32[1,1,1,4096]{3,2,1,0:T(1,128)S(1)}, f32[1,1,1,4096]{3,2,1,0:T(1,128)}, u32[]{:S(2)}) copy-start(f32[1,1,1,4096]{3,2,1,0:T(1,128)} %get-tuple-element.322) | copy-start | bytes 49156
  519.0 23.3 %copy-start.99 = (f32[1,1,1,4096]{3,2,1,0:T(1,128)S(1)}, f32[1,1,1,4096]{3,2,1,0:T(1,128)}, u32[]{:S(2)}) copy-start(f32[1,1,1,4096]{3,2,1,0:T(1,128)} %get-tuple-element.323) | copy-start | bytes 49156
  519.0 23.3 %copy-start.100 = (f32[1,1,1,4096]{3,2,1,0:T(1,128)S(1)}, f32[1,1,1,4096]{3,2,1,0:T(1,128)}, u32[]{:S(2)}) copy-start(f32[1,1,1,4096]{3,2,1,0:T(1,128)} %get-tuple-element.324) | copy-start | bytes 49156
  519.0 23.3 %copy-start.101 = (f32[1,1,1,4096]{3,2,1,0:T(1,128)S(1)}, f32[1,1,1,4096]{3,2,1,0:T(1,128)}, u32[]{:S(2)}) copy-start(f32[1,1,1,4096]{3,2,1,0:T(1,128)} %get-tuple-element.325) | copy-start | bytes 49156
  519.0 23.3 %copy-start.102 = (f32[1,1,1,4096]{3,2,1,0:T(1,128)S(1)}, f32[1,1,1,4096]{3,2,1,0:T(1,128)}, u32[]{:S(2)}) copy-start(f32[1,1,1,4096]{3,2,1,0:T(1,128)} %get-tuple-element.326) | copy-start | bytes 49156
  519.1 23.3 %copy-start.103 = (f32[1,1,1,4096]{3,2,1,0:T(1,128)S(1)}, f32[1,1,1,4096]{3,2,1,0:T(1,128)}, u32[]{:S(2)}) copy-start(f32[1,1,1,4096]{3,2,1,0:T(1,128)} %get-tuple-element.327) | copy-start | bytes 49156
  519.1 23.3 %copy-start.104 = (f32[1,1,1,4096]{3,2,1,0:T(1,128)S(1)}, f32[1,1,1,4096]{3,2,1,0:T(1,128)}, u32[]{:S(2)}) copy-start(f32[1,1,1,4096]{3,2,1,0:T(1,128)} %get-tuple-element.328) | copy-start | bytes 49156
  519.1 24.3 %copy-start.1 = (f32[9,9,9]{2,1,0:T(8,128)S(1)}, f32[9,9,9]{2,1,0:T(8,128)}, u32[]{:S(2)}) copy-start(f32[9,9,9]{2,1,0:T(8,128)} %param.11) | copy-start | bytes 8752
  (85 other events, 592.4 us)
where the time goes:
time: 554 us; the launch traced here: 544 us
  local copies, waits for them, and re-layouts  262 us (47%)
  other arithmetic  191 us (34%)
  matrix products  40.5 us (7%)
  waiting for transfers between devices  24.1 us (4%)
  starting transfers between devices  22.1 us (4%)
    gather x8, local copies, waits for them, and re-layouts, per_device(): flat_potential[corner_ids[corner]][None]  184 us
    scatter-add x1, other arithmetic, per_device(): jax.ops.segment_sum(spread_values.reshape(-1), jnp.stack(corner_ids).resh...  171 us
    dot_general x27, matrix products, convolve(): jnp.dot(joined.reshape(block_rows * block_cols, KERNEL * z_size), tables[...  33.6 us
    slice x30, local copies, waits for them, and re-layouts, convolve(): tables[shift_x]  26.9 us
    concatenate x19, local copies, waits for them, and re-layouts, convolve(): jnp.concatenate([x_slab[:, shift_y:shift_y + block_cols, :] for shift_y i...  15.6 us
    unnamed x239, local copies, waits for them, and re-layouts  13 us
    ppermute x8, starting transfers between devices, from_behind(): return lax.ppermute(value, axis, pairs)  12.2 us
    ppermute x8, waiting for transfers between devices, from_behind(): return lax.ppermute(value, axis, pairs)  11.2 us
  transfers between devices with their start and end apart: 20, of which 10 were waited for; matrix products, arithmetic and copies ran while one was open for 17% of the time, Pallas kernels for 0%

commit v1 on v0

v1 whole, which is shorter than its diff:
```python
import jax
import jax.numpy as jnp
from jax import lax
from jax.experimental import pallas as pl
from jax.experimental.pallas import tpu as pltpu
from jax.sharding import PartitionSpec as P

CX = 16
CY = 24
NZ = 128
KERNEL = 9
HALF = KERNEL // 2
LANES = 128
CHUNK = 512
MESH = pl.DeviceIdType.MESH

BX = (CX, CX // 2, CX // 4)
BY = (CY, CY // 2, CY // 4)
RY = tuple(-(-(size + 1) // 8) * 8 for size in BY)
ZS = (NZ, NZ // 2, NZ // 4)
COARSE_LANE = ZS[1]


def split(value):
    high = value.astype(jnp.bfloat16)
    return high, (value - high.astype(jnp.float32)).astype(jnp.bfloat16)


def matmul(a, b):
    return jnp.dot(a, b, preferred_element_type=jnp.float32)


def matmul_nt(a, b):
    return lax.dot_general(a, b, (((1,), (1,)), ((), ())), preferred_element_type=jnp.float32)


def exact(a, b):
    return jnp.dot(a, b, preferred_element_type=jnp.float32, precision=lax.Precision.HIGHEST)


def hat(distance):
    return jnp.maximum(1.0 - jnp.abs(distance), 0.0)


def ring_hat(distance, period):
    distance = jnp.abs(distance)
    return jnp.maximum(1.0 - jnp.minimum(distance, period - distance), 0.0)


def rows_iota(rows, columns):
    return lax.broadcasted_iota(jnp.int32, (rows, columns), 0)


def bases(cell):
    return cell // (CY * NZ), (cell // NZ) % CY, cell % NZ


def spread_kernel(count_ref, cell_ref, frac_ref, charge_ref, fine_ref, strip_ref, middle_ref, coarse_ref):
    slots = cell_ref.shape[1]
    fine = jnp.zeros((fine_ref.shape[0] * RY[0], LANES), jnp.float32)
    rest = jnp.zeros(((BX[1] + 1) * RY[1] + (BX[2] + 1) * RY[2], LANES), jnp.float32)
    for start in range(0, slots, CHUNK):
        part = slice(start, start + CHUNK)
        base = bases(cell_ref[:, part])
        place = [base[k].astype(jnp.float32) + frac_ref[k : k + 1, part] for k in range(3)]
        slot = start + lax.broadcasted_iota(jnp.int32, (1, CHUNK), 1)
        charge = jnp.where(slot < count_ref[0, 0], charge_ref[:, part], 0.0)
        tops = []
        for level in range(3):
            scale = 0.5**level
            row_x = rows_iota(-(-(BX[level] + 1) // 8) * 8, CHUNK).astype(jnp.float32)
            row_y = rows_iota(RY[level], CHUNK).astype(jnp.float32)
            weight_x = hat(place[0] * scale - row_x) * charge
            weight_y = hat(place[1] * scale - row_y)
            tops.append(
                jnp.concatenate([weight_x[x : x + 1] * weight_y for x in range(BX[level] + 1)], axis=0)
            )
        z_fine = ring_hat(place[2] - rows_iota(NZ, CHUNK).astype(jnp.float32), float(NZ))
        z_middle = ring_hat(place[2] * 0.5 - rows_iota(ZS[1], CHUNK).astype(jnp.float32), float(ZS[1]))
        z_coarse = ring_hat(place[2] * 0.25 - rows_iota(ZS[2], CHUNK).astype(jnp.float32), float(ZS[2]))
        z_rest = jnp.concatenate([z_middle, z_coarse, jnp.zeros_like(z_coarse)], axis=0)
        for which, top, z_side in ((0, tops[0], z_fine), (1, jnp.concatenate(tops[1:], axis=0), z_rest)):
            top_high, top_low = split(top)
            z_high, z_low = split(z_side)
            both = matmul_nt(top_high, jnp.concatenate([z_high, z_low], axis=0))
            term = both[:, :LANES] + both[:, LANES:] + matmul_nt(top_low, z_high)
            if which == 0:
                fine = fine + term
            else:
                rest = rest + term
    fine = fine.reshape(BX[0] + 1, RY[0], LANES)
    fine_ref[...] = fine
    strip_ref[...] = fine[:, BY[0] - HALF : BY[0] - HALF + 8, :]
    rows = (BX[1] + 1) * RY[1]
    middle_ref[...] = rest[:rows].reshape(BX[1] + 1, RY[1], LANES)
    coarse_ref[...] = rest[rows:].reshape(BX[2] + 1, RY[2], LANES)


def transfers():
    plans = []
    for level in range(3):
        far = 2 if level == 2 else 1
        for dx in range(-far, far + 1):
            for dy in (-1, 0, 1):
                if dx == 0 and dy == 0:
                    continue
                low_x = max(0, dx * BX[level] - HALF)
                high_x = min(BX[level] + 1, dx * BX[level] + BX[level] + HALF + 1)
                source = level
                low_y, size_y = 0, RY[level]
                shift = 0
                if level == 0 and dy == 1:
                    source, low_y, size_y, shift = 3, 0, 8, BY[0] - HALF
                elif level < 2 and dy == -1:
                    size_y = 8
                elif level == 1 and dy == 1:
                    low_y, size_y = 8, 8
                at_x = low_x - dx * BX[level]
                at_y = low_y + shift - dy * BY[level]
                plans.append((level, dx, dy, source, low_x, high_x - low_x, low_y, size_y, at_x, at_y))
    return plans


PLANS = transfers()


def exchange_kernel(sizes, *refs):
    sources = refs[:4]
    targets = refs[4 : 4 + len(PLANS)]
    send_sem, recv_sem = refs[4 + len(PLANS) :]
    me = (lax.axis_index("gx"), lax.axis_index("gy"))

    def device(dx, dy):
        return (lax.rem(me[0] + dx + sizes[0], sizes[0]), lax.rem(me[1] + dy + sizes[1], sizes[1]))

    barrier = pltpu.get_barrier_semaphore()
    around = sorted({(plan[1], plan[2]) for plan in PLANS})
    for dx, dy in around:
        pl.semaphore_signal(barrier, inc=1, device_id=device(dx, dy), device_id_type=MESH)
    pl.semaphore_wait(barrier, len(around))
    copies = []
    for index, (_, dx, dy, source, low_x, size_x, low_y, size_y, _, _) in enumerate(PLANS):
        copies.append(
            pltpu.make_async_remote_copy(
                src_ref=sources[source].at[pl.ds(low_x, size_x), pl.ds(low_y, size_y)],
                dst_ref=targets[index],
                send_sem=send_sem.at[index],
                recv_sem=recv_sem.at[index],
                device_id=device(dx, dy),
                device_id_type=MESH,
            )
        )
    for copy in copies:
        copy.start()
    for copy in copies:
        copy.wait()


def build_tables(kernel_ref, high_ref, low_ref, z_size, z_from_lane):
    packed = LANES // z_size
    blocks = -(-KERNEL // packed)
    row = rows_iota(8, LANES)
    lane = lax.broadcasted_iota(jnp.int32, (8, LANES), 1)
    tap = lax.rem(row - lane + HALF + 2 * LANES, z_size)

    def step(shift_x, carry):
        for block in range(blocks):
            for inner in range(packed):
                shift_y = block * packed + inner
                top = jnp.zeros((8, LANES), jnp.float32)
                if shift_y < KERNEL:
                    for c in range(KERNEL):
                        value = kernel_ref[shift_x, shift_y * KERNEL + c]
                        top = jnp.where(tap == c, value, top)
                pieces = [top]
                for piece in range(1, z_size // 8):
                    pieces.append(pltpu.roll(top, 8 * piece, 1))
                table_high, table_low = split(jnp.concatenate(pieces, axis=0))
                place = slice(block * LANES + inner * z_size, block * LANES + (inner + 1) * z_size)
                high_ref[shift_x, place, :] = table_high
                low_ref[shift_x, place, :] = table_low
        return carry

    lax.fori_loop(0, KERNEL, step, 0)


def pack_taps(padded, z_size, rows):
    packed = LANES // z_size
    group = lax.broadcasted_iota(jnp.int32, (1, 1, LANES), 2) // z_size
    blocks = []
    for block in range(-(-KERNEL // packed)):
        value = padded[:, block * packed : block * packed + rows, :]
        for inner in range(1, packed):
            first = block * packed + inner
            if first < KERNEL:
                value = jnp.where(group == inner, padded[:, first : first + rows, :], value)
        blocks.append(value)
    return blocks


def potential_kernel(*refs):
    kernels = refs[:3]
    own = refs[3:6]
    arrived = refs[6 : 6 + len(PLANS)]
    out_ref = refs[6 + len(PLANS)]
    scratch = refs[7 + len(PLANS) :]
    padded_refs, table_refs, joined_refs = scratch[:3], scratch[3:9], scratch[9:15]
    results = []
    for level in (2, 1, 0):
        x_out, rows = BX[level] + 1, RY[level]
        padded = padded_refs[level]
        padded[...] = jnp.zeros_like(padded)
        padded[HALF : HALF + x_out, 8 : 8 + rows, :] = own[level][...]
        for index, plan in enumerate(PLANS):
            if plan[0] == level:
                size_x, size_y, at_x, at_y = plan[5], plan[7], plan[8], plan[9]
                xs = slice(HALF + at_x, HALF + at_x + size_x)
                ys = slice(8 + at_y, 8 + at_y + size_y)
                padded[xs, ys, :] = padded[xs, ys, :] + arrived[index][...]
        high_table, low_table = table_refs[2 * level], table_refs[2 * level + 1]
        build_tables(kernels[level], high_table, low_table, ZS[level], 0)
        joined_high, joined_low = joined_refs[2 * level], joined_refs[2 * level + 1]
        copied = LANES // ZS[level]
        whole = padded[:, HALF : HALF + rows + KERNEL - 1 + copied, :]
        if level > 0:
            first = 0 if level == 1 else COARSE_LANE
            lanes = lax.broadcasted_iota(jnp.int32, (1, 1, LANES), 2)
            whole = jnp.where((lanes >= first) & (lanes < first + ZS[level]), whole, 0.0)
            shape = whole.shape
            flat = whole.reshape(shape[0] * shape[1], LANES)
            source = rows_iota(LANES, LANES)
            target = lax.broadcasted_iota(jnp.int32, (LANES, LANES), 1)
            repeat = (lax.rem(target, ZS[level]) + first == source).astype(jnp.float32)
            whole = exact(flat, repeat).reshape(shape)
        for block, value in enumerate(pack_taps(whole, ZS[level], rows)):
            value_high, value_low = split(value)
            joined_high[:, :, block * LANES : (block + 1) * LANES] = value_high
            joined_low[:, :, block * LANES : (block + 1) * LANES] = value_low
        total = jnp.zeros((x_out * rows, LANES), jnp.float32)
        for shift_x in range(KERNEL):
            left_high = joined_high[shift_x : shift_x + x_out].reshape(x_out * rows, -1)
            left_low = joined_low[shift_x : shift_x + x_out].reshape(x_out * rows, -1)
            total = total + matmul(left_high, high_table[shift_x])
            total = total + matmul(left_low, high_table[shift_x])
            total = total + matmul(left_high, low_table[shift_x])
        if level < 2:
            below = results[-1]
            z_low = rows_iota(LANES, LANES)
            lane = lax.broadcasted_iota(jnp.int32, (LANES, LANES), 1)
            lane = lax.rem(lane, ZS[level])
            z_weight = ring_hat(lane.astype(jnp.float32) * 0.5 - z_low.astype(jnp.float32), float(ZS[level + 1]))
            z_weight = jnp.where(z_low < ZS[level + 1], z_weight, 0.0)
            below = exact(below, z_weight)
            rows_below = RY[level + 1]
            count_below = (BX[level + 1] + 1) * rows_below
            fine_row = rows_iota(x_out * rows, count_below)
            low_row = lax.broadcasted_iota(jnp.int32, (x_out * rows, count_below), 1)
            weight = hat((fine_row // rows).astype(jnp.float32) * 0.5 - (low_row // rows_below).astype(jnp.float32))
            weight = weight * hat(
                lax.rem(fine_row, rows).astype(jnp.float32) * 0.5 - lax.rem(low_row, rows_below).astype(jnp.float32)
            )
            total = total + exact(weight, below)
        results.append(total)
    out_ref[...] = results[-1].reshape(BX[0] + 1, RY[0], LANES)


def force_kernel(count_ref, cell_ref, frac_ref, charge_ref, potential_ref, forces_ref):
    slots = cell_ref.shape[1]
    rows = RY[0]
    grid_in = potential_ref[...].reshape((BX[0] + 1) * rows, LANES)
    left = jnp.concatenate(split(grid_in), axis=1)
    for start in range(0, slots, CHUNK):
        part = slice(start, start + CHUNK)
        base_x, base_y, base_z = bases(cell_ref[:, part])
        frac = [frac_ref[k : k + 1, part] for k in range(3)]
        slot = start + lax.broadcasted_iota(jnp.int32, (1, CHUNK), 1)
        charge = jnp.where(slot < count_ref[0, 0], charge_ref[:, part], 0.0)
        row_z = rows_iota(NZ, CHUNK)
        pick_low = jnp.where(row_z == base_z, 1.0, 0.0).astype(jnp.bfloat16)
        pick_high = jnp.where(row_z == lax.rem(base_z + 1, NZ), 1.0, 0.0).astype(jnp.bfloat16)
        low = matmul(left, jnp.concatenate([pick_low, pick_low], axis=0))
        high = matmul(left, jnp.concatenate([pick_high, pick_high], axis=0))
        slope = high - low
        level = low + frac[2] * slope
        row_x = rows_iota(-(-(BX[0] + 1) // 8) * 8, CHUNK)
        row_y = rows_iota(rows, CHUNK)

        def sides(row, base, f):
            lower, upper = row == base, row == base + 1
            weight = jnp.where(lower, 1.0 - f, jnp.where(upper, f, 0.0))
            sign = jnp.where(lower, -1.0, jnp.where(upper, 1.0, 0.0))
            return weight, sign

        weight_x, sign_x = sides(row_x, base_x, frac[0])
        weight_y, sign_y = sides(row_y, base_y, frac[1])
        in_x = jnp.zeros((rows, CHUNK), jnp.float32)
        across_x = jnp.zeros((rows, CHUNK), jnp.float32)
        in_z = jnp.zeros((rows, CHUNK), jnp.float32)
        for x in range(BX[0] + 1):
            piece = level[x * rows : (x + 1) * rows]
            in_x = in_x + weight_x[x : x + 1] * piece
            across_x = across_x + sign_x[x : x + 1] * piece
            in_z = in_z + weight_x[x : x + 1] * slope[x * rows : (x + 1) * rows]
        forces_ref[0:1, part] = -charge * jnp.sum(weight_y * across_x, axis=0, keepdims=True)
        forces_ref[1:2, part] = -charge * jnp.sum(sign_y * in_x, axis=0, keepdims=True)
        forces_ref[2:3, part] = -charge * jnp.sum(weight_y * in_z, axis=0, keepdims=True)


VMEM = pl.BlockSpec(memory_space=pltpu.VMEM)
SMEM = pl.BlockSpec(memory_space=pltpu.SMEM)


def grid_shape(level):
    return jax.ShapeDtypeStruct((BX[level] + 1, RY[level], LANES), jnp.float32)


def solution(mesh):
    sizes = (mesh.shape["gx"], mesh.shape["gy"])

    def per_device(atom_cell, atom_frac, atom_charge, atom_count, fine_kernel, middle_kernel, coarse_kernel):
        slots = atom_cell.shape[-1]
        cell = atom_cell.reshape(1, slots)
        frac = atom_frac.reshape(3, slots)
        charge = atom_charge.reshape(1, slots)
        raw = pl.pallas_call(
            spread_kernel,
            out_shape=(
                grid_shape(0),
                jax.ShapeDtypeStruct((BX[0] + 1, 8, LANES), jnp.float32),
                grid_shape(1),
                grid_shape(2),
            ),
            in_specs=[SMEM, VMEM, VMEM, VMEM],
            out_specs=(VMEM,) * 4,
            name="spread",
        )(atom_count, cell, frac, charge)
        fine, strip, middle, coarse = raw
        arrived = pl.pallas_call(
            lambda *refs: exchange_kernel(sizes, *refs),
            out_shape=tuple(jax.ShapeDtypeStruct((plan[5], plan[7], LANES), jnp.float32) for plan in PLANS),
            in_specs=[VMEM] * 4,
            out_specs=(VMEM,) * len(PLANS),
            scratch_shapes=[
                pltpu.SemaphoreType.DMA((len(PLANS),)),
                pltpu.SemaphoreType.DMA((len(PLANS),)),
            ],
            compiler_params=pltpu.CompilerParams(collective_id=0, has_side_effects=True),
            name="exchange",
        )(fine, middle, coarse, strip)
        kernels = [k.reshape(KERNEL, KERNEL * KERNEL) for k in (fine_kernel, middle_kernel, coarse_kernel)]
        padded_shapes, table_shapes, joined_shapes = [], [], []
        for level in range(3):
            packed = LANES // ZS[level]
            depth = -(-KERNEL // packed) * LANES
            x_in = BX[level] + KERNEL
            padded_shapes.append(pltpu.VMEM((x_in, RY[level] + 24, LANES), jnp.float32))
            table_shapes += [pltpu.VMEM((KERNEL, depth, LANES), jnp.bfloat16)] * 2
            joined_shapes += [pltpu.VMEM((x_in, RY[level], depth), jnp.bfloat16)] * 2
        extended = pl.pallas_call(
            potential_kernel,
            out_shape=grid_shape(0),
            in_specs=[SMEM] * 3 + [VMEM] * (3 + len(PLANS)),
            out_specs=VMEM,
            scratch_shapes=padded_shapes + table_shapes + joined_shapes,
            name="potential",
        )(*kernels, fine, middle, coarse, *arrived)
        forces = pl.pallas_call(
            force_kernel,
            out_shape=jax.ShapeDtypeStruct((3, slots), jnp.float32),
            in_specs=[SMEM, VMEM, VMEM, VMEM, VMEM],
            out_specs=VMEM,
            name="forces",
        )(atom_count, cell, frac, charge, extended)
        return extended[:CX, :CY], forces.reshape(3, 1, 1, slots)

    return jax.shard_map(
        per_device,
        mesh=mesh,
        in_specs=(
            P("gx", "gy", None),
            P(None, "gx", "gy", None),
            P("gx", "gy", None),
            P("gx", "gy"),
            P(),
            P(),
            P(),
        ),
        out_specs=(P("gx", "gy", None), P(None, "gx", "gy", None)),
        check_vma=False,
    )
```

time: 554 us -> 59.7 us (0.11); the launches traced: 544 us -> 59.3 us
  local copies, waits for them, and re-layouts: 262 us -> 5.27 us
  other arithmetic: 191 us -> 0 us
  Pallas kernels: 0 us -> 52.7 us
  matrix products: 40.5 us -> 0 us
  waiting for transfers between devices: 24.1 us -> 0 us
  starting transfers between devices: 22.1 us -> 0 us
    gather x8 -> x0, local copies, waits for them, and re-layouts: 184 us -> none  [per_device(): flat_potential[corner_ids[corner]][None]]
    scatter-add x1 -> x0, other arithmetic: 171 us -> none  [per_device(): jax.ops.segment_sum(spread_values.reshape(-1), jnp.stack(corner_ids).resh...]
    pallas_call x0 -> x4, Pallas kernels: none -> 52.7 us  [the longest x1 20.9 us: per_device(): pl.pallas_call(potential_kernel, out_shape=grid_shape(0), in_specs=[SMEM]...]
    dot_general x30 -> x0, matrix products: 40.5 us -> none  [the longest x27 33.6 us: convolve(): jnp.dot(joined.reshape(block_rows * block_cols, KERNEL * z_size), tables[...]
    slice x63 -> x1, local copies, waits for them, and re-layouts: 38.3 us -> 0.69 us  [per_device(): return (extended[:CX, :CY], forces.reshape(3, 1, 1, slots))]
    ppermute x20 -> x0, waiting for transfers between devices: 24.1 us -> none  [the longest x8 11.2 us: from_behind(): return lax.ppermute(value, axis, pairs)]
    ppermute x20 -> x0, starting transfers between devices: 22.1 us -> none  [the longest x8 12.2 us: from_behind(): return lax.ppermute(value, axis, pairs)]
    concatenate x20 -> x0, local copies, waits for them, and re-layouts: 15.6 us -> none  [the longest x19 15.6 us: convolve(): jnp.concatenate([x_slab[:, shift_y:shift_y + block_cols, :] for shift_y i...]
  transfers between devices with their start and end apart: 20 -> 0, of which waited for: 10 -> 0; matrix products, arithmetic and copies ran while one was open for 17% -> 0% of each run, Pallas kernels for 0% -> 0%
where the time goes in v1:
time: 59.7 us; the launch traced here: 59.3 us
  Pallas kernels  52.7 us (88%)
  local copies, waits for them, and re-layouts  5.27 us (9%)
  between operations  1.35 us (2%)
    pallas_call x1, Pallas kernels, per_device(): pl.pallas_call(potential_kernel, out_shape=grid_shape(0), in_specs=[SMEM]...  20.9 us
    pallas_call x1, Pallas kernels, per_device(): pl.pallas_call(lambda *refs: exchange_kernel(sizes, *refs), out_shape=tup...  20.2 us
    pallas_call x1, Pallas kernels, per_device(): pl.pallas_call(force_kernel, out_shape=jax.ShapeDtypeStruct((3, slots), j...  6.34 us
    pallas_call x1, Pallas kernels, per_device(): pl.pallas_call(spread_kernel, out_shape=(grid_shape(0), jax.ShapeDtypeStr...  5.36 us
    reshape x3, local copies, waits for them, and re-layouts, per_device(): k.reshape(KERNEL, KERNEL * KERNEL)  2.96 us
    unnamed x12, local copies, waits for them, and re-layouts  1.62 us

profile of v1, /device:TPU:0, one launch (start us, length us, event | category | flops | bytes accessed | tf_op | source)
XLA Modules:
  0.0 59.3 jit_solution(18420835920313196761)
XLA Ops:
  0.6 0.0 copy-start.2
  1.3 0.0 copy-start.3
  1.3 1.6 %reshape.25.refs_0_ = f32[9,81]{1,0:T(8,128)} reshape(f32[9,9,9]{2,1,0:T(8,128)} %param.11) | data formatting | bytes 5832 | tf_op jit(solution)/shard_map/reshape | solution.py:350
  2.9 0.0 copy-done.2
  2.9 0.7 %reshape.26.refs_1_ = f32[9,81]{1,0:T(8,128)} reshape(f32[9,9,9]{2,1,0:T(8,128)S(1)} %copy-done.2) | data formatting | bytes 5832 | tf_op jit(solution)/shard_map/reshape | solution.py:350
  3.6 0.0 copy-done.3
  3.6 0.0 copy-start.4
  3.6 0.7 %reshape.27.refs_2_ = f32[9,81]{1,0:T(8,128)} reshape(f32[9,9,9]{2,1,0:T(8,128)S(1)} %copy-done.3) | data formatting | bytes 5832 | tf_op jit(solution)/shard_map/reshape | solution.py:350
  4.3 0.1 copy-done.4
  4.4 0.7 %copy.12 = f32[3,1,1,4096]{3,0,1,2:T(4,128)} copy(f32[3,1,1,4096]{3,2,1,0:T(1,128)S(1)} %copy-done.4) | data formatting | bytes 98304
  5.1 5.4 %spread.1 = (f32[17,32,128]{2,1,0:T(8,128)}, f32[17,8,128]{2,1,0:T(8,128)}, f32[9,16,128]{2,1,0:T(8,128)}, f32[5,8,128]{2,1,0:T(8,128)}) custom-call(s32[1,1]{1,0:T(1,128)S(6)} %copy.13.count_ref, s32[1,4096]{1,0:T(1,128)} %bitcast.9, f32[3,4096]{1,0:T(4,128)} %bitcast.6, f32[1,4096]{1,0:T(1,128)} %bitcast.11), custom_call_target="tpu_custom_call" | custom-call | tf_op jit(solution)/shard_map/spread/pallas_call | solution.py:325
  10.4 20.2 %exchange.1 = (f32[5,8,128]{2,1,0:T(8,128)}, f32[5,32,128]{2,1,0:T(8,128)}, f32[5,8,128]{2,1,0:T(8,128)}, f32[17,8,128]{2,1,0:T(8,128)}, f32[17,8,128]{2,1,0:T(8...) custom-call(f32[17,32,128]{2,1,0:T(8,128)} %get-tuple-element.36.ref, ...), custom_call_target="tpu_custom_call" | custom-call | tf_op jit(solution)/shard_map/exchange/pallas_call | solution.py:338
  30.6 20.9 %potential.1.potential_ref = f32[17,32,128]{2,1,0:T(8,128)} custom-call(f32[9,81]{1,0:T(8,128)} %reshape.25.refs_0_, f32[9,81]{1,0:T(8,128)} %reshape.26.refs_1_, f32[9,81]{1,0:T(8,128)} %reshape.27.refs_2_, f32[17,32,128]{2,1,0:T(8,128)} %get-tuple-element.36.refs_0_.refs_3_, f32[9,16,128]{2,1,0:T(8,128)} %get-tuple-element.37.refs_1_.refs_4_, ...), custom_call_target="tpu_custom_call" | custom-call | tf_op jit(solution)/shard_map/potential/pallas_call | solution.py:359
  51.5 0.0 copy-start
  51.5 6.3 %forces.1 = f32[3,4096]{1,0:T(4,128)} custom-call(s32[1,1]{1,0:T(1,128)S(6)} %copy.13.count_ref, s32[1,4096]{1,0:T(1,128)} %bitcast.10, f32[3,4096]{1,0:T(4,128)} %bitcast.7, f32[1,4096]{1,0:T(1,128)} %bitcast.12, f32[17,32,128]{2,1,0:T(8,128)} %potential.1.potential_ref), custom_call_target="tpu_custom_call" | custom-call | tf_op jit(solution)/shard_map/forces/pallas_call | solution.py:367
  57.8 0.0 copy-done
  57.8 0.0 copy-start.1
  57.8 0.7 %slice.4 = f32[16,24,128]{2,1,0:T(8,128)} slice(f32[17,32,128]{2,1,0:T(8,128)S(1)} %copy-done), slice={[0:16], [0:24], [0:128]} | slice | bytes 393216 | tf_op jit(solution)/shard_map/slice | solution.py:374
  58.5 0.1 copy-done.1
  58.7 0.7 %copy.9 = f32[3,1,1,4096]{3,2,1,0:T(1,128)} copy(f32[3,1,1,4096]{3,0,2,1:T(4,128)S(1)} %bitcast.8) | data formatting | bytes 98304
Async XLA Ops:
  0.6 2.3 %copy-start.2 = (f32[9,9,9]{2,1,0:T(8,128)S(1)}, f32[9,9,9]{2,1,0:T(8,128)}, u32[]{:S(2)}) copy-start(f32[9,9,9]{2,1,0:T(8,128)} %param.12) | copy-start | bytes 8752
  1.3 2.3 %copy-start.3 = (f32[9,9,9]{2,1,0:T(8,128)S(1)}, f32[9,9,9]{2,1,0:T(8,128)}, u32[]{:S(2)}) copy-start(f32[9,9,9]{2,1,0:T(8,128)} %param.13) | copy-start | bytes 8752
  3.6 0.8 %copy-start.4 = (f32[3,1,1,4096]{3,2,1,0:T(1,128)S(1)}, f32[3,1,1,4096]{3,2,1,0:T(1,128)}, u32[]{:S(2)}) copy-start(f32[3,1,1,4096]{3,2,1,0:T(1,128)} %param.8) | copy-start | bytes 147460
  51.5 6.4 %copy-start = (f32[17,32,128]{2,1,0:T(8,128)S(1)}, f32[17,32,128]{2,1,0:T(8,128)}, u32[]{:S(2)}) copy-start(f32[17,32,128]{2,1,0:T(8,128)} %potential.1.potential_ref) | copy-start | bytes 835588
  57.8 0.8 %copy-start.1 = (f32[3,4096]{1,0:T(4,128)S(1)}, f32[3,4096]{1,0:T(4,128)}, u32[]{:S(2)}) copy-start(f32[3,4096]{1,0:T(4,128)} %forces.1) | copy-start | bytes 147460

commit v2 on v1

--- a/solution.py
+++ b/solution.py
@@ -56,15 +56,15 @@
 
 
 def spread_kernel(count_ref, cell_ref, frac_ref, charge_ref, fine_ref, strip_ref, middle_ref, coarse_ref):
-    slots = cell_ref.shape[1]
+    slots = cell_ref.shape[-1]
     fine = jnp.zeros((fine_ref.shape[0] * RY[0], LANES), jnp.float32)
     rest = jnp.zeros(((BX[1] + 1) * RY[1] + (BX[2] + 1) * RY[2], LANES), jnp.float32)
     for start in range(0, slots, CHUNK):
         part = slice(start, start + CHUNK)
-        base = bases(cell_ref[:, part])
-        place = [base[k].astype(jnp.float32) + frac_ref[k : k + 1, part] for k in range(3)]
+        base = bases(cell_ref[0, :, part])
+        place = [base[k].astype(jnp.float32) + frac_ref[k, 0, :, part] for k in range(3)]
         slot = start + lax.broadcasted_iota(jnp.int32, (1, CHUNK), 1)
-        charge = jnp.where(slot < count_ref[0, 0], charge_ref[:, part], 0.0)
+        charge = jnp.where(slot < count_ref[0, 0], charge_ref[0, :, part], 0.0)
         tops = []
         for level in range(3):
             scale = 0.5**level
@@ -124,10 +124,7 @@
 PLANS = transfers()
 
 
-def exchange_kernel(sizes, *refs):
-    sources = refs[:4]
-    targets = refs[4 : 4 + len(PLANS)]
-    send_sem, recv_sem = refs[4 + len(PLANS) :]
+def halo_copies(sizes, sources, targets, send_sem, recv_sem):
     me = (lax.axis_index("gx"), lax.axis_index("gy"))
 
     def device(dx, dy):
@@ -150,13 +147,10 @@
                 device_id_type=MESH,
             )
         )
-    for copy in copies:
-        copy.start()
-    for copy in copies:
-        copy.wait()
-
-
-def build_tables(kernel_ref, high_ref, low_ref, z_size, z_from_lane):
+    return copies
+
+
+def build_tables(kernel_ref, high_ref, low_ref, z_size, pair):
     packed = LANES // z_size
     blocks = -(-KERNEL // packed)
     row = rows_iota(8, LANES)
@@ -170,15 +164,18 @@
                 top = jnp.zeros((8, LANES), jnp.float32)
                 if shift_y < KERNEL:
                     for c in range(KERNEL):
-                        value = kernel_ref[shift_x, shift_y * KERNEL + c]
+                        value = kernel_ref[shift_x, shift_y, c]
                         top = jnp.where(tap == c, value, top)
                 pieces = [top]
                 for piece in range(1, z_size // 8):
                     pieces.append(pltpu.roll(top, 8 * piece, 1))
                 table_high, table_low = split(jnp.concatenate(pieces, axis=0))
                 place = slice(block * LANES + inner * z_size, block * LANES + (inner + 1) * z_size)
-                high_ref[shift_x, place, :] = table_high
-                low_ref[shift_x, place, :] = table_low
+                high_ref[shift_x, place, :LANES] = table_high
+                low_ref[shift_x, place, :LANES] = table_low
+                if pair:
+                    high_ref[shift_x + 1, place, LANES:] = table_high
+                    low_ref[shift_x + 1, place, LANES:] = table_low
         return carry
 
     lax.fori_loop(0, KERNEL, step, 0)
@@ -198,19 +195,36 @@
     return blocks
 
 
-def potential_kernel(*refs):
+def potential_kernel(sizes, *refs):
     kernels = refs[:3]
-    own = refs[3:6]
-    arrived = refs[6 : 6 + len(PLANS)]
-    out_ref = refs[6 + len(PLANS)]
-    scratch = refs[7 + len(PLANS) :]
+    sources = refs[3:7]
+    out_ref, whole_ref = refs[7:9]
+    scratch = refs[9:]
     padded_refs, table_refs, joined_refs = scratch[:3], scratch[3:9], scratch[9:15]
+    arrived = scratch[15 : 15 + len(PLANS)]
+    send_sem, recv_sem = scratch[15 + len(PLANS) :]
+    copies = halo_copies(sizes, sources, arrived, send_sem, recv_sem)
+    for level in (2, 1, 0):
+        for index, plan in enumerate(PLANS):
+            if plan[0] == level:
+                copies[index].start()
+    for level in (2, 1, 0):
+        build_tables(kernels[level], table_refs[2 * level], table_refs[2 * level + 1], ZS[level], level == 0)
+        padded_refs[level][...] = jnp.zeros_like(padded_refs[level])
+        padded_refs[level][HALF : HALF + BX[level] + 1, 8 : 8 + RY[level], :] = sources[level][...]
+    if True:
+        high_table, low_table = table_refs[:2]
+        high_table[0, :, LANES:] = jnp.zeros_like(high_table[0, :, LANES:])
+        low_table[0, :, LANES:] = jnp.zeros_like(low_table[0, :, LANES:])
+        high_table[KERNEL, :, :LANES] = jnp.zeros_like(high_table[0, :, LANES:])
+        low_table[KERNEL, :, :LANES] = jnp.zeros_like(low_table[0, :, LANES:])
     results = []
     for level in (2, 1, 0):
         x_out, rows = BX[level] + 1, RY[level]
         padded = padded_refs[level]
-        padded[...] = jnp.zeros_like(padded)
-        padded[HALF : HALF + x_out, 8 : 8 + rows, :] = own[level][...]
+        for index, plan in enumerate(PLANS):
+            if plan[0] == level:
+                copies[index].wait()
         for index, plan in enumerate(PLANS):
             if plan[0] == level:
                 size_x, size_y, at_x, at_y = plan[5], plan[7], plan[8], plan[9]
@@ -218,7 +232,6 @@
                 ys = slice(8 + at_y, 8 + at_y + size_y)
                 padded[xs, ys, :] = padded[xs, ys, :] + arrived[index][...]
         high_table, low_table = table_refs[2 * level], table_refs[2 * level + 1]
-        build_tables(kernels[level], high_table, low_table, ZS[level], 0)
         joined_high, joined_low = joined_refs[2 * level], joined_refs[2 * level + 1]
         copied = LANES // ZS[level]
         whole = padded[:, HALF : HALF + rows + KERNEL - 1 + copied, :]
@@ -226,23 +239,36 @@
             first = 0 if level == 1 else COARSE_LANE
             lanes = lax.broadcasted_iota(jnp.int32, (1, 1, LANES), 2)
             whole = jnp.where((lanes >= first) & (lanes < first + ZS[level]), whole, 0.0)
-            shape = whole.shape
-            flat = whole.reshape(shape[0] * shape[1], LANES)
-            source = rows_iota(LANES, LANES)
-            target = lax.broadcasted_iota(jnp.int32, (LANES, LANES), 1)
-            repeat = (lax.rem(target, ZS[level]) + first == source).astype(jnp.float32)
-            whole = exact(flat, repeat).reshape(shape)
+            spread_out = whole
+            for turn in range(1, copied):
+                spread_out = spread_out + pltpu.roll(whole, turn * ZS[level], 2)
+            whole = spread_out
         for block, value in enumerate(pack_taps(whole, ZS[level], rows)):
             value_high, value_low = split(value)
             joined_high[:, :, block * LANES : (block + 1) * LANES] = value_high
             joined_low[:, :, block * LANES : (block + 1) * LANES] = value_low
-        total = jnp.zeros((x_out * rows, LANES), jnp.float32)
-        for shift_x in range(KERNEL):
-            left_high = joined_high[shift_x : shift_x + x_out].reshape(x_out * rows, -1)
-            left_low = joined_low[shift_x : shift_x + x_out].reshape(x_out * rows, -1)
-            total = total + matmul(left_high, high_table[shift_x])
-            total = total + matmul(left_low, high_table[shift_x])
-            total = total + matmul(left_high, low_table[shift_x])
+        if level > 0:
+            total = jnp.zeros((x_out * rows, LANES), jnp.float32)
+            for shift_x in range(KERNEL):
+                left_high = joined_high[shift_x : shift_x + x_out].reshape(x_out * rows, -1)
+                left_low = joined_low[shift_x : shift_x + x_out].reshape(x_out * rows, -1)
+                total = total + matmul(left_high, high_table[shift_x])
+                total = total + matmul(left_low, high_table[shift_x])
+                total = total + matmul(left_high, low_table[shift_x])
+        else:
+            pairs = (x_out + 1) // 2
+            by_pair = [
+                ref.reshape(ref.shape[0] // 2, 2, ref.shape[1], ref.shape[2]) for ref in (joined_high, joined_low)
+            ]
+            both = jnp.zeros((pairs * rows, 2 * LANES), jnp.float32)
+            for shift_x in range(KERNEL + 1):
+                left_high, left_low = [
+                    ref[shift_x // 2 : shift_x // 2 + pairs, shift_x % 2].reshape(pairs * rows, -1) for ref in by_pair
+                ]
+                both = both + matmul(left_high, high_table[shift_x])
+                both = both + matmul(left_low, high_table[shift_x])
+                both = both + matmul(left_high, low_table[shift_x])
+            total = 0.0
         if level < 2:
             below = results[-1]
             z_low = rows_iota(LANES, LANES)
@@ -261,20 +287,26 @@
             )
             total = total + exact(weight, below)
         results.append(total)
-    out_ref[...] = results[-1].reshape(BX[0] + 1, RY[0], LANES)
+    rows = RY[0]
+    for x in range(BX[0] + 1):
+        piece = results[-1][x * rows : (x + 1) * rows]
+        piece = piece + both[(x // 2) * rows : (x // 2 + 1) * rows, (x % 2) * LANES : (x % 2 + 1) * LANES]
+        whole_ref[x] = piece
+        if x < BX[0]:
+            out_ref[x] = piece[: BY[0]]
 
 
 def force_kernel(count_ref, cell_ref, frac_ref, charge_ref, potential_ref, forces_ref):
-    slots = cell_ref.shape[1]
+    slots = cell_ref.shape[-1]
     rows = RY[0]
     grid_in = potential_ref[...].reshape((BX[0] + 1) * rows, LANES)
     left = jnp.concatenate(split(grid_in), axis=1)
     for start in range(0, slots, CHUNK):
         part = slice(start, start + CHUNK)
-        base_x, base_y, base_z = bases(cell_ref[:, part])
-        frac = [frac_ref[k : k + 1, part] for k in range(3)]
+        base_x, base_y, base_z = bases(cell_ref[0, :, part])
+        frac = [frac_ref[k, 0, :, part] for k in range(3)]
         slot = start + lax.broadcasted_iota(jnp.int32, (1, CHUNK), 1)
-        charge = jnp.where(slot < count_ref[0, 0], charge_ref[:, part], 0.0)
+        charge = jnp.where(slot < count_ref[0, 0], charge_ref[0, :, part], 0.0)
         row_z = rows_iota(NZ, CHUNK)
         pick_low = jnp.where(row_z == base_z, 1.0, 0.0).astype(jnp.bfloat16)
         pick_high = jnp.where(row_z == lax.rem(base_z + 1, NZ), 1.0, 0.0).astype(jnp.bfloat16)
@@ -301,9 +333,9 @@
             in_x = in_x + weight_x[x : x + 1] * piece
             across_x = across_x + sign_x[x : x + 1] * piece
             in_z = in_z + weight_x[x : x + 1] * slope[x * rows : (x + 1) * rows]
-        forces_ref[0:1, part] = -charge * jnp.sum(weight_y * across_x, axis=0, keepdims=True)
-        forces_ref[1:2, part] = -charge * jnp.sum(sign_y * in_x, axis=0, keepdims=True)
-        forces_ref[2:3, part] = -charge * jnp.sum(weight_y * in_z, axis=0, keepdims=True)
+        forces_ref[0, 0, :, part] = -charge * jnp.sum(weight_y * across_x, axis=0, keepdims=True)
+        forces_ref[1, 0, :, part] = -charge * jnp.sum(sign_y * in_x, axis=0, keepdims=True)
+        forces_ref[2, 0, :, part] = -charge * jnp.sum(weight_y * in_z, axis=0, keepdims=True)
 
 
 VMEM = pl.BlockSpec(memory_space=pltpu.VMEM)
@@ -319,9 +351,6 @@
 
     def per_device(atom_cell, atom_frac, atom_charge, atom_count, fine_kernel, middle_kernel, coarse_kernel):
         slots = atom_cell.shape[-1]
-        cell = atom_cell.reshape(1, slots)
-        frac = atom_frac.reshape(3, slots)
-        charge = atom_charge.reshape(1, slots)
         raw = pl.pallas_call(
             spread_kernel,
             out_shape=(
@@ -333,45 +362,35 @@
             in_specs=[SMEM, VMEM, VMEM, VMEM],
             out_specs=(VMEM,) * 4,
             name="spread",
-        )(atom_count, cell, frac, charge)
+        )(atom_count, atom_cell, atom_frac, atom_charge)
         fine, strip, middle, coarse = raw
-        arrived = pl.pallas_call(
-            lambda *refs: exchange_kernel(sizes, *refs),
-            out_shape=tuple(jax.ShapeDtypeStruct((plan[5], plan[7], LANES), jnp.float32) for plan in PLANS),
-            in_specs=[VMEM] * 4,
-            out_specs=(VMEM,) * len(PLANS),
-            scratch_shapes=[
-                pltpu.SemaphoreType.DMA((len(PLANS),)),
-                pltpu.SemaphoreType.DMA((len(PLANS),)),
-            ],
-            compiler_params=pltpu.CompilerParams(collective_id=0, has_side_effects=True),
-            name="exchange",
-        )(fine, middle, coarse, strip)
-        kernels = [k.reshape(KERNEL, KERNEL * KERNEL) for k in (fine_kernel, middle_kernel, coarse_kernel)]
         padded_shapes, table_shapes, joined_shapes = [], [], []
         for level in range(3):
             packed = LANES // ZS[level]
             depth = -(-KERNEL // packed) * LANES
-            x_in = BX[level] + KERNEL
+            x_in = BX[level] + KERNEL + (level == 0)
+            width = 2 * LANES if level == 0 else LANES
             padded_shapes.append(pltpu.VMEM((x_in, RY[level] + 24, LANES), jnp.float32))
-            table_shapes += [pltpu.VMEM((KERNEL, depth, LANES), jnp.bfloat16)] * 2
+            table_shapes += [pltpu.VMEM((KERNEL + (level == 0), depth, width), jnp.bfloat16)] * 2
             joined_shapes += [pltpu.VMEM((x_in, RY[level], depth), jnp.bfloat16)] * 2
-        extended = pl.pallas_call(
-            potential_kernel,
-            out_shape=grid_shape(0),
-            in_specs=[SMEM] * 3 + [VMEM] * (3 + len(PLANS)),
-            out_specs=VMEM,
-            scratch_shapes=padded_shapes + table_shapes + joined_shapes,
+        landing = [pltpu.VMEM((plan[5], plan[7], LANES), jnp.float32) for plan in PLANS]
+        potential, extended = pl.pallas_call(
+            lambda *refs: potential_kernel(sizes, *refs),
+            out_shape=(jax.ShapeDtypeStruct((CX, CY, NZ), jnp.float32), grid_shape(0)),
+            in_specs=[SMEM] * 3 + [VMEM] * 4,
+            out_specs=(VMEM, VMEM),
+            scratch_shapes=padded_shapes + table_shapes + joined_shapes + landing + [pltpu.SemaphoreType.DMA((len(PLANS),))] * 2,
+            compiler_params=pltpu.CompilerParams(collective_id=0, has_side_effects=True),
             name="potential",
-        )(*kernels, fine, middle, coarse, *arrived)
+        )(fine_kernel, middle_kernel, coarse_kernel, fine, middle, coarse, strip)
         forces = pl.pallas_call(
             force_kernel,
-            out_shape=jax.ShapeDtypeStruct((3, slots), jnp.float32),
+            out_shape=jax.ShapeDtypeStruct((3, 1, 1, slots), jnp.float32),
             in_specs=[SMEM, VMEM, VMEM, VMEM, VMEM],
             out_specs=VMEM,
             name="forces",
-        )(atom_count, cell, frac, charge, extended)
-        return extended[:CX, :CY], forces.reshape(3, 1, 1, slots)
+        )(atom_count, atom_cell, atom_frac, atom_charge, extended)
+        return potential, forces
 
     return jax.shard_map(
         per_device,

time: 59.7 us -> 44.1 us (0.74)
  Pallas kernels: 52.7 us -> 41.9 us
  local copies, waits for them, and re-layouts: 5.27 us -> 0.68 us
    pallas_call x3 -> x2, Pallas kernels: 47.4 us -> 36.6 us  [the longest x1 30.2 us: per_device(): pl.pallas_call(lambda *refs: potential_kernel(sizes, *refs), out_shape=(j...]
    reshape x3 -> x0, local copies, waits for them, and re-layouts: 2.96 us -> none  [per_device(): k.reshape(KERNEL, KERNEL * KERNEL)]
    unnamed x12 -> x3, local copies, waits for them, and re-layouts: 1.62 us -> 0.68 us
    slice x1 -> x0, local copies, waits for them, and re-layouts: 0.69 us -> none  [per_device(): return (extended[:CX, :CY], forces.reshape(3, 1, 1, slots))]
where the time goes in v2:
time: 44.1 us; the launch traced here: 43.9 us
  Pallas kernels  41.9 us (95%)
  between operations  1.29 us (3%)
  local copies, waits for them, and re-layouts  0.68 us (2%)
    pallas_call x1, Pallas kernels, per_device(): pl.pallas_call(lambda *refs: potential_kernel(sizes, *refs), out_shape=(j...  30.2 us
    pallas_call x1, Pallas kernels, per_device(): pl.pallas_call(force_kernel, out_shape=jax.ShapeDtypeStruct((3, 1, 1, slo...  6.33 us
    pallas_call x1, Pallas kernels, per_device(): pl.pallas_call(spread_kernel, out_shape=(grid_shape(0), jax.ShapeDtypeStr...  5.31 us

profile of v2, /device:TPU:0, one launch (start us, length us, event | category | flops | bytes accessed | tf_op | source)
XLA Modules:
  0.0 43.9 jit_solution(18287862102830825521)
XLA Ops:
  1.3 5.3 %spread.1 = (f32[17,32,128]{2,1,0:T(8,128)}, f32[17,8,128]{2,1,0:T(8,128)}, f32[9,16,128]{2,1,0:T(8,128)}, f32[5,8,128]{2,1,0:T(8,128)}) custom-call(s32[1,1]{1,0:T(1,128)S(6)} %copy.10.count_ref, s32[1,1,4096]{2,1,0:T(1,128)} %cell_ref.3, f32[3,1,1,4096]{3,2,1,0:T(1,128)} %frac_ref.3, f32[1,1,4096]{2,1,0:T(1,128)} %charge_ref.3), custom_call_target="tpu_custom_call" | custom-call | tf_op jit(solution)/shard_map/spread/pallas_call | solution.py:354
  6.6 30.2 %potential.1 = (f32[16,24,128]{2,1,0:T(8,128)}, f32[17,32,128]{2,1,0:T(8,128)}) custom-call(f32[9,9,9]{2,1,0:T(8,128)} %refs_0_.1, f32[9,9,9]{2,1,0:T(8,128)} %refs_1_.1, f32[9,9,9]{2,1,0:T(8,128)} %refs_2_.1, f32[17,32,128]{2,1,0:T(8,128)} %get-tuple-element.8.refs_3_, f32[9,16,128]{2,1,0:T(8,128)} %get-tuple-element.9.refs_4_, ...), custom_call_target="tpu_custom_call" | custom-call | tf_op jit(solution)/shard_map/potential/pallas_call | solution.py:377
  36.8 0.0 copy-start
  36.9 6.3 %forces.1 = f32[3,1,1,4096]{3,2,1,0:T(1,128)} custom-call(s32[1,1]{1,0:T(1,128)S(6)} %copy.10.count_ref, s32[1,1,4096]{2,1,0:T(1,128)} %cell_ref.3, f32[3,1,1,4096]{3,2,1,0:T(1,128)} %frac_ref.3, f32[1,1,4096]{2,1,0:T(1,128)} %charge_ref.3, f32[17,32,128]{2,1,0:T(8,128)} %get-tuple-element.13.potential_ref), custom_call_target="tpu_custom_call" | custom-call | tf_op jit(solution)/shard_map/forces/pallas_call | solution.py:386
  43.2 0.0 copy-done
  43.2 0.7 %copy.11 = f32[16,24,128]{2,1,0:T(8,128)} copy(f32[16,24,128]{2,1,0:T(8,128)S(1)} %copy-done) | data formatting | bytes 393216
Async XLA Ops:
  36.8 6.3 %copy-start = (f32[16,24,128]{2,1,0:T(8,128)S(1)}, f32[16,24,128]{2,1,0:T(8,128)}, u32[]{:S(2)}) copy-start(f32[16,24,128]{2,1,0:T(8,128)} %get-tuple-element.16) | copy-start | bytes 589828

commit v3 on v2

--- a/solution.py
+++ b/solution.py
@@ -55,7 +55,7 @@
     return cell // (CY * NZ), (cell // NZ) % CY, cell % NZ
 
 
-def spread_kernel(count_ref, cell_ref, frac_ref, charge_ref, fine_ref, strip_ref, middle_ref, coarse_ref):
+def spread_kernel(count_ref, cell_ref, frac_ref, charge_ref, fine_ref, strip_ref, middle_ref, upper_ref, coarse_ref):
     slots = cell_ref.shape[-1]
     fine = jnp.zeros((fine_ref.shape[0] * RY[0], LANES), jnp.float32)
     rest = jnp.zeros(((BX[1] + 1) * RY[1] + (BX[2] + 1) * RY[2], LANES), jnp.float32)
@@ -92,36 +92,56 @@
     fine_ref[...] = fine
     strip_ref[...] = fine[:, BY[0] - HALF : BY[0] - HALF + 8, :]
     rows = (BX[1] + 1) * RY[1]
-    middle_ref[...] = rest[:rows].reshape(BX[1] + 1, RY[1], LANES)
-    coarse_ref[...] = rest[rows:].reshape(BX[2] + 1, RY[2], LANES)
+    middle = rest[:rows].reshape(BX[1] + 1, RY[1], LANES)
+    coarse = rest[rows:].reshape(BX[2] + 1, RY[2], LANES)
+    coarse_ref[...] = coarse
+    lane = lax.broadcasted_iota(jnp.int32, (1, 1, LANES), 2)
+    twice = jnp.concatenate([coarse, coarse], axis=1)
+    x_coarse = BX[2] + 1
+    top = BX[1] + 1 - x_coarse
+    middle_ref[:top] = middle[:top]
+    middle_ref[top:] = jnp.where(lane < COARSE_LANE, middle[top:], twice)
+    upper_ref[...] = jnp.where(lane < COARSE_LANE, middle[:x_coarse], twice)
+    for x in range(HALF + 1):
+        middle_ref[top + x, RY[1] - 1 : RY[1], :] = fine[BX[0] - HALF + x, BY[0] : BY[0] + 1, :]
+        upper_ref[x, RY[1] - 1 : RY[1], :] = fine[x, BY[0] : BY[0] + 1, :]
 
 
 def transfers():
-    plans = []
-    for level in range(3):
-        far = 2 if level == 2 else 1
-        for dx in range(-far, far + 1):
-            for dy in (-1, 0, 1):
-                if dx == 0 and dy == 0:
-                    continue
-                low_x = max(0, dx * BX[level] - HALF)
-                high_x = min(BX[level] + 1, dx * BX[level] + BX[level] + HALF + 1)
-                source = level
-                low_y, size_y = 0, RY[level]
-                shift = 0
-                if level == 0 and dy == 1:
-                    source, low_y, size_y, shift = 3, 0, 8, BY[0] - HALF
-                elif level < 2 and dy == -1:
-                    size_y = 8
-                elif level == 1 and dy == 1:
-                    low_y, size_y = 8, 8
-                at_x = low_x - dx * BX[level]
-                at_y = low_y + shift - dy * BY[level]
-                plans.append((level, dx, dy, source, low_x, high_x - low_x, low_y, size_y, at_x, at_y))
-    return plans
-
-
-PLANS = transfers()
+    plans, adds = [], ([], [], [])
+    reach = HALF + 1
+    for dx in (-2, 2):
+        for dy in (-1, 0, 1):
+            low = 0 if dx < 0 else BX[2]
+            adds[2].append((len(plans), 0, 1, 0, RY[2], low - dx * BX[2], -dy * BY[2]))
+            plans.append((dx, dy, 2, low, 1, 0, RY[2]))
+    for dx in (-1, 0, 1):
+        for dy in (-1, 0, 1):
+            if dx == 0 and dy == 0:
+                continue
+            low, size = {-1: (0, reach), 0: (0, BX[1] + 1), 1: (BX[1] - HALF, reach)}[dx]
+            low_y, size_y, used = {-1: (0, 8, reach), 0: (0, RY[1], BY[1] + 1), 1: (BY[1] - HALF, 8, reach)}[dy]
+            index = len(plans)
+            adds[1].append((index, 0, size, 0, used, low - dx * BX[1], low_y - dy * BY[1]))
+            ride = BX[1] - HALF if dx == 0 else 0
+            adds[2].append((index, ride, BX[2] + 1, 0, BY[2] + 1, -dx * BX[2], -dy * BY[2]))
+            if dx != 0 and dy == 0:
+                low_x = 0 if dx < 0 else BX[0] - HALF
+                adds[0].append((index, 0, reach, RY[1] - 1, 1, low_x - dx * BX[0], BY[0]))
+            plans.append((dx, dy, 4 if dx < 0 else 1, low, size, low_y, size_y))
+    for dx in (-1, 0, 1):
+        for dy in (-1, 0, 1):
+            if dx == 0 and dy == 0:
+                continue
+            low, size = {-1: (0, reach), 0: (0, BX[0] + 1), 1: (BX[0] - HALF, reach)}[dx]
+            source, size_y, first_y = {-1: (0, 8, 0), 0: (0, BY[0], 0), 1: (3, 8, BY[0] - HALF)}[dy]
+            used = min(size_y, reach) if dy else size_y
+            adds[0].append((len(plans), 0, size, 0, used, low - dx * BX[0], first_y - dy * BY[0]))
+            plans.append((dx, dy, source, low, size, 0, size_y))
+    return plans, adds
+
+
+PLANS, ADDS = transfers()
 
 
 def halo_copies(sizes, sources, targets, send_sem, recv_sem):
@@ -131,12 +151,12 @@
         return (lax.rem(me[0] + dx + sizes[0], sizes[0]), lax.rem(me[1] + dy + sizes[1], sizes[1]))
 
     barrier = pltpu.get_barrier_semaphore()
-    around = sorted({(plan[1], plan[2]) for plan in PLANS})
+    around = sorted({plan[:2] for plan in PLANS})
     for dx, dy in around:
         pl.semaphore_signal(barrier, inc=1, device_id=device(dx, dy), device_id_type=MESH)
     pl.semaphore_wait(barrier, len(around))
     copies = []
-    for index, (_, dx, dy, source, low_x, size_x, low_y, size_y, _, _) in enumerate(PLANS):
+    for index, (dx, dy, source, low_x, size_x, low_y, size_y) in enumerate(PLANS):
         copies.append(
             pltpu.make_async_remote_copy(
                 src_ref=sources[source].at[pl.ds(low_x, size_x), pl.ds(low_y, size_y)],
@@ -186,32 +206,31 @@
     group = lax.broadcasted_iota(jnp.int32, (1, 1, LANES), 2) // z_size
     blocks = []
     for block in range(-(-KERNEL // packed)):
-        value = padded[:, block * packed : block * packed + rows, :]
+        value = padded[:, HALF + block * packed : HALF + block * packed + rows, :]
         for inner in range(1, packed):
             first = block * packed + inner
             if first < KERNEL:
-                value = jnp.where(group == inner, padded[:, first : first + rows, :], value)
+                value = jnp.where(group == inner, padded[:, HALF + first : HALF + first + rows, :], value)
         blocks.append(value)
     return blocks
 
 
 def potential_kernel(sizes, *refs):
     kernels = refs[:3]
-    sources = refs[3:7]
-    out_ref, whole_ref = refs[7:9]
-    scratch = refs[9:]
+    sources = refs[3:8]
+    out_ref, whole_ref = refs[8:10]
+    scratch = refs[10:]
     padded_refs, table_refs, joined_refs = scratch[:3], scratch[3:9], scratch[9:15]
     arrived = scratch[15 : 15 + len(PLANS)]
-    send_sem, recv_sem = scratch[15 + len(PLANS) :]
+    send_sem, recv_sem, raised_ref = scratch[15 + len(PLANS) :]
     copies = halo_copies(sizes, sources, arrived, send_sem, recv_sem)
-    for level in (2, 1, 0):
-        for index, plan in enumerate(PLANS):
-            if plan[0] == level:
-                copies[index].start()
+    for copy in copies:
+        copy.start()
     for level in (2, 1, 0):
         build_tables(kernels[level], table_refs[2 * level], table_refs[2 * level + 1], ZS[level], level == 0)
         padded_refs[level][...] = jnp.zeros_like(padded_refs[level])
-        padded_refs[level][HALF : HALF + BX[level] + 1, 8 : 8 + RY[level], :] = sources[level][...]
+        used = BY[level] + 1
+        padded_refs[level][HALF : HALF + BX[level] + 1, 8 : 8 + used, :] = sources[level][:, :used, :]
     if True:
         high_table, low_table = table_refs[:2]
         high_table[0, :, LANES:] = jnp.zeros_like(high_table[0, :, LANES:])
@@ -219,31 +238,51 @@
         high_table[KERNEL, :, :LANES] = jnp.zeros_like(high_table[0, :, LANES:])
         low_table[KERNEL, :, :LANES] = jnp.zeros_like(low_table[0, :, LANES:])
     results = []
+    waited = set()
     for level in (2, 1, 0):
         x_out, rows = BX[level] + 1, RY[level]
         padded = padded_refs[level]
-        for index, plan in enumerate(PLANS):
-            if plan[0] == level:
+        if level < 2:
+            below = results[-1]
+            z_low = rows_iota(LANES, LANES)
+            lane = lax.broadcasted_iota(jnp.int32, (LANES, LANES), 1)
+            lane = lax.rem(lane, ZS[level])
+            z_weight = ring_hat(lane.astype(jnp.float32) * 0.5 - z_low.astype(jnp.float32), float(ZS[level + 1]))
+            z_weight = jnp.where(z_low < ZS[level + 1], z_weight, 0.0)
+            below = exact(below, z_weight)
+            rows_below = RY[level + 1]
+            count_below = (BX[level + 1] + 1) * rows_below
+            fine_row = rows_iota(x_out * rows, count_below)
+            low_row = lax.broadcasted_iota(jnp.int32, (x_out * rows, count_below), 1)
+            weight = hat((fine_row // rows).astype(jnp.float32) * 0.5 - (low_row // rows_below).astype(jnp.float32))
+            weight = weight * hat(
+                lax.rem(fine_row, rows).astype(jnp.float32) * 0.5 - lax.rem(low_row, rows_below).astype(jnp.float32)
+            )
+            raised = exact(weight, below)
+            if level == 0:
+                raised_ref[...] = raised
+        for index in sorted({add[0] for add in ADDS[level]}):
+            if index not in waited:
                 copies[index].wait()
-        for index, plan in enumerate(PLANS):
-            if plan[0] == level:
-                size_x, size_y, at_x, at_y = plan[5], plan[7], plan[8], plan[9]
-                xs = slice(HALF + at_x, HALF + at_x + size_x)
-                ys = slice(8 + at_y, 8 + at_y + size_y)
-                padded[xs, ys, :] = padded[xs, ys, :] + arrived[index][...]
+                waited.add(index)
+        for index, from_x, size_x, from_y, size_y, at_x, at_y in ADDS[level]:
+            xs = slice(HALF + at_x, HALF + at_x + size_x)
+            ys = slice(8 + at_y, 8 + at_y + size_y)
+            piece = arrived[index][from_x : from_x + size_x, from_y : from_y + size_y, :]
+            padded[xs, ys, :] = padded[xs, ys, :] + piece
         high_table, low_table = table_refs[2 * level], table_refs[2 * level + 1]
         joined_high, joined_low = joined_refs[2 * level], joined_refs[2 * level + 1]
         copied = LANES // ZS[level]
-        whole = padded[:, HALF : HALF + rows + KERNEL - 1 + copied, :]
         if level > 0:
+            whole = padded[...]
             first = 0 if level == 1 else COARSE_LANE
             lanes = lax.broadcasted_iota(jnp.int32, (1, 1, LANES), 2)
             whole = jnp.where((lanes >= first) & (lanes < first + ZS[level]), whole, 0.0)
             spread_out = whole
             for turn in range(1, copied):
                 spread_out = spread_out + pltpu.roll(whole, turn * ZS[level], 2)
-            whole = spread_out
-        for block, value in enumerate(pack_taps(whole, ZS[level], rows)):
+            padded[...] = spread_out
+        for block, value in enumerate(pack_taps(padded, ZS[level], rows)):
             value_high, value_low = split(value)
             joined_high[:, :, block * LANES : (block + 1) * LANES] = value_high
             joined_low[:, :, block * LANES : (block + 1) * LANES] = value_low
@@ -268,28 +307,13 @@
                 both = both + matmul(left_high, high_table[shift_x])
                 both = both + matmul(left_low, high_table[shift_x])
                 both = both + matmul(left_high, low_table[shift_x])
-            total = 0.0
-        if level < 2:
-            below = results[-1]
-            z_low = rows_iota(LANES, LANES)
-            lane = lax.broadcasted_iota(jnp.int32, (LANES, LANES), 1)
-            lane = lax.rem(lane, ZS[level])
-            z_weight = ring_hat(lane.astype(jnp.float32) * 0.5 - z_low.astype(jnp.float32), float(ZS[level + 1]))
-            z_weight = jnp.where(z_low < ZS[level + 1], z_weight, 0.0)
-            below = exact(below, z_weight)
-            rows_below = RY[level + 1]
-            count_below = (BX[level + 1] + 1) * rows_below
-            fine_row = rows_iota(x_out * rows, count_below)
-            low_row = lax.broadcasted_iota(jnp.int32, (x_out * rows, count_below), 1)
-            weight = hat((fine_row // rows).astype(jnp.float32) * 0.5 - (low_row // rows_below).astype(jnp.float32))
-            weight = weight * hat(
-                lax.rem(fine_row, rows).astype(jnp.float32) * 0.5 - lax.rem(low_row, rows_below).astype(jnp.float32)
-            )
-            total = total + exact(weight, below)
+            total = None
+        if level == 1:
+            total = total + raised
         results.append(total)
     rows = RY[0]
     for x in range(BX[0] + 1):
-        piece = results[-1][x * rows : (x + 1) * rows]
+        piece = raised_ref[x * rows : (x + 1) * rows]
         piece = piece + both[(x // 2) * rows : (x // 2 + 1) * rows, (x % 2) * LANES : (x % 2 + 1) * LANES]
         whole_ref[x] = piece
         if x < BX[0]:
@@ -357,13 +381,14 @@
                 grid_shape(0),
                 jax.ShapeDtypeStruct((BX[0] + 1, 8, LANES), jnp.float32),
                 grid_shape(1),
+                jax.ShapeDtypeStruct((BX[2] + 1, RY[1], LANES), jnp.float32),
                 grid_shape(2),
             ),
             in_specs=[SMEM, VMEM, VMEM, VMEM],
-            out_specs=(VMEM,) * 4,
+            out_specs=(VMEM,) * 5,
             name="spread",
         )(atom_count, atom_cell, atom_frac, atom_charge)
-        fine, strip, middle, coarse = raw
+        fine, strip, middle, upper, coarse = raw
         padded_shapes, table_shapes, joined_shapes = [], [], []
         for level in range(3):
             packed = LANES // ZS[level]
@@ -373,16 +398,21 @@
             padded_shapes.append(pltpu.VMEM((x_in, RY[level] + 24, LANES), jnp.float32))
             table_shapes += [pltpu.VMEM((KERNEL + (level == 0), depth, width), jnp.bfloat16)] * 2
             joined_shapes += [pltpu.VMEM((x_in, RY[level], depth), jnp.bfloat16)] * 2
-        landing = [pltpu.VMEM((plan[5], plan[7], LANES), jnp.float32) for plan in PLANS]
+        landing = [pltpu.VMEM((plan[4], plan[6], LANES), jnp.float32) for plan in PLANS]
         potential, extended = pl.pallas_call(
             lambda *refs: potential_kernel(sizes, *refs),
             out_shape=(jax.ShapeDtypeStruct((CX, CY, NZ), jnp.float32), grid_shape(0)),
-            in_specs=[SMEM] * 3 + [VMEM] * 4,
+            in_specs=[SMEM] * 3 + [VMEM] * 5,
             out_specs=(VMEM, VMEM),
-            scratch_shapes=padded_shapes + table_shapes + joined_shapes + landing + [pltpu.SemaphoreType.DMA((len(PLANS),))] * 2,
+            scratch_shapes=padded_shapes
+            + table_shapes
+            + joined_shapes
+            + landing
+            + [pltpu.SemaphoreType.DMA((len(PLANS),))] * 2
+            + [pltpu.VMEM(((BX[0] + 1) * RY[0], LANES), jnp.float32)],
             compiler_params=pltpu.CompilerParams(collective_id=0, has_side_effects=True),
             name="potential",
-        )(fine_kernel, middle_kernel, coarse_kernel, fine, middle, coarse, strip)
+        )(fine_kernel, middle_kernel, coarse_kernel, fine, middle, coarse, strip, upper)
         forces = pl.pallas_call(
             force_kernel,
             out_shape=jax.ShapeDtypeStruct((3, 1, 1, slots), jnp.float32),

time: 44.1 us -> 41.7 us (0.946)
  Pallas kernels: 41.9 us -> 39.3 us
    pallas_call x1, Pallas kernels: 30.2 us -> 27.7 us  [per_device(): pl.pallas_call(lambda *refs: potential_kernel(sizes, *refs), out_shape=(j...]
where the time goes in v3:
time: 41.7 us; the launch traced here: 41.3 us
  Pallas kernels  39.3 us (94%)
  between operations  1.29 us (3%)
  local copies, waits for them, and re-layouts  0.68 us (2%)
    pallas_call x1, Pallas kernels, per_device(): pl.pallas_call(lambda *refs: potential_kernel(sizes, *refs), out_shape=(j...  27.7 us
    pallas_call x1, Pallas kernels, per_device(): pl.pallas_call(force_kernel, out_shape=jax.ShapeDtypeStruct((3, 1, 1, slo...  6.33 us
    pallas_call x1, Pallas kernels, per_device(): pl.pallas_call(spread_kernel, out_shape=(grid_shape(0), jax.ShapeDtypeStr...  5.31 us

profile of v3, /device:TPU:0, one launch (start us, length us, event | category | flops | bytes accessed | tf_op | source)
XLA Modules:
  0.0 41.3 jit_solution(15005304560862169188)
XLA Ops:
  1.3 5.3 %spread.1 = (f32[17,32,128]{2,1,0:T(8,128)}, f32[17,8,128]{2,1,0:T(8,128)}, f32[9,16,128]{2,1,0:T(8,128)}, f32[5,16,128]{2,1,0:T(8,128)}, f32[5,8,128]{2,1,0:T(8,128)}) custom-call(s32[1,1]{1,0:T(1,128)S(6)} %copy.10.count_ref, s32[1,1,4096]{2,1,0:T(1,128)} %cell_ref.3, f32[3,1,1,4096]{3,2,1,0:T(1,128)} %frac_ref.3, f32[1,1,4096]{2,1,0:T(1,128)} %charge_ref.3), custom_call_target="tpu_custom_call" | custom-call | tf_op jit(solution)/shard_map/spread/pallas_call | solution.py:378
  6.6 27.7 %potential.1 = (f32[16,24,128]{2,1,0:T(8,128)}, f32[17,32,128]{2,1,0:T(8,128)}) custom-call(f32[9,9,9]{2,1,0:T(8,128)} %refs_0_.1, f32[9,9,9]{2,1,0:T(8,128)} %refs_1_.1, f32[9,9,9]{2,1,0:T(8,128)} %refs_2_.1, f32[17,32,128]{2,1,0:T(8,128)} %get-tuple-element.9.refs_3_, f32[9,16,128]{2,1,0:T(8,128)} %get-tuple-element.10.refs_4_, ...), custom_call_target="tpu_custom_call" | custom-call | tf_op jit(solution)/shard_map/potential/pallas_call | solution.py:402
  34.3 0.0 copy-start
  34.3 6.3 %forces.1 = f32[3,1,1,4096]{3,2,1,0:T(1,128)} custom-call(s32[1,1]{1,0:T(1,128)S(6)} %copy.10.count_ref, s32[1,1,4096]{2,1,0:T(1,128)} %cell_ref.3, f32[3,1,1,4096]{3,2,1,0:T(1,128)} %frac_ref.3, f32[1,1,4096]{2,1,0:T(1,128)} %charge_ref.3, f32[17,32,128]{2,1,0:T(8,128)} %get-tuple-element.15.potential_ref), custom_call_target="tpu_custom_call" | custom-call | tf_op jit(solution)/shard_map/forces/pallas_call | solution.py:416
  40.6 0.0 copy-done
  40.6 0.7 %copy.11 = f32[16,24,128]{2,1,0:T(8,128)} copy(f32[16,24,128]{2,1,0:T(8,128)S(1)} %copy-done) | data formatting | bytes 393216
Async XLA Ops:
  34.3 6.3 %copy-start = (f32[16,24,128]{2,1,0:T(8,128)S(1)}, f32[16,24,128]{2,1,0:T(8,128)}, u32[]{:S(2)}) copy-start(f32[16,24,128]{2,1,0:T(8,128)} %get-tuple-element.18) | copy-start | bytes 589828
